TPU v7x, 128 devices: a whole 4x4x4 slice. The times are simulated.
128 devices in a mesh: row: 8 (over x_hi, y), col: 16 (over z, x_lo, core).
Axes of the slice: x: 4 (x_hi: 2, x_lo: 2; x = x_hi * 2 + x_lo), y: 4, z: 4, core: 2. Of those that a mesh axis runs over, the one named last changes fastest.
Arguments:
- pair_ints: bfloat16 [2048, 16384], P(None, ('row', 'col')), may hold values from -0.59765625 to 0.59765625
- denominators: float32 [2048], replicated, may hold values from 0.5 to 4
- lap_points: float32 [3], replicated, may hold values from 0.05 to 1.5
- lap_weights: float32 [3], replicated, may hold values from 0.2 to 1
Outputs:
- aux_matrices: float32 [3, 16384, 16384], P(None, 'row', 'col')
All inputs are finite; a program needn't handle non-finite values.
Results may differ from a plain program's by a relative error of at most 0.0027.
Values may be sent and summed in bfloat16 or wider, within the bound.
A program may use at most 128 MiB of HBM per device.

v0:
```python
import jax
import jax.numpy as jnp
from jax import lax
from jax.sharding import PartitionSpec as P


def on_device(pair_ints, denominators, lap_points, lap_weights):
    factors = lap_weights[:, None] * jnp.exp(-lap_points[:, None] * denominators[None, :])
    pair_rows = lax.all_to_all(pair_ints, ("row", "col"), split_axis=0, concat_axis=1, tiled=True)
    col_block = lax.all_to_all(pair_rows, "col", split_axis=1, concat_axis=0, tiled=True)
    col_whole = lax.all_gather(col_block, "row", axis=0, tiled=True)
    weighted = (
        lax.all_gather(pair_ints, "col", axis=1, tiled=True).astype(jnp.float32)[None]
        * factors[:, :, None]
    ).astype(jnp.bfloat16)
    return jnp.einsum("trp,rq->tpq", weighted, col_whole, preferred_element_type=jnp.float32)


def solution(mesh):
    in_specs = (P(None, ("row", "col")), P(), P(), P())
    out_specs = P(None, "row", "col")
    return jax.shard_map(
        on_device, mesh=mesh, in_specs=in_specs, out_specs=out_specs, check_vma=False
    )
```

profile of v0, /device:TPU:36, one launch (start us, length us, event | category | flops | bytes accessed | tf_op | source)
XLA Modules:
  0.0 193.7 jit_solution(1863049342206637796)
XLA Ops:
  6.5 0.0 all-gather.3.cloned.1.call-start
  6.5 0.7 all-gather.3.cloned.1.call-update
  7.3 0.0 all-gather.5.cloned.1.call-start
  7.3 23.0 %all_to_all.35 = bf16[128,16,128]{2,1,0:T(8,128)(2,1)S(1)} all-to-all(bf16[128,16,128]{2,1,0:T(8,128)(2,1)} %bitcast.8), channel_id=1, replica_groups=mesh['row'=8,'col'=16] {'row','col'}, dimensions={0} | all-to-all | bytes 1048576 | tf_op jit(solution)/shard_map/all_to_all | solution.py:9
  30.3 0.1 copy.10
  30.5 0.2 all_to_all.29
  30.7 0.3 copy.11
  31.0 18.9 %all_to_all.36 = bf16[16,16,1024]{2,0,1:T(8,128)(2,1)} all-to-all(bf16[16,16,1024]{2,0,1:T(8,128)(2,1)S(1)} %copy.11), channel_id=1, replica_groups=mesh['row'=8,'col'=16] {'col'}, dimensions={1} | all-to-all | bytes 1048576 | tf_op jit(solution)/shard_map/all_to_all | solution.py:10
  49.9 0.0 all-gather.5.cloned.1.call-update
  50.0 0.7 neg.4
  50.6 0.8 exponential_multiply_fusion
  51.4 30.5 %all-gather.3.cloned.1.call-done = bf16[2048,2048]{1,0:T(8,128)(2,1)} async-done(((bf16[2048,128]{1,0:T(8,128)(2,1)}), bf16[2048,2048]{1,0:T(8,128)(2,1)}) %all-gather.3.cloned.1.call-update) | async-done | bytes 8388624 | tf_op jit(solution)/shard_map/all_gather | solution.py:13
  81.9 13.0 %copy.9 = f32[2048,2048]{0,1:T(8,128)} copy(bf16[2048,2048]{1,0:T(8,128)(2,1)} %all-gather.3.cloned.1.call-done) | data formatting | bytes 25165824 | tf_op jit(solution)/shard_map/convert_element_type | solution.py:13
  94.9 58.4 %all-gather.5.cloned.1.call-done = bf16[2048,1024]{1,0:T(8,128)(2,1)} async-done(((bf16[256,1024]{1,0:T(8,128)(2,1)}), bf16[2048,1024]{1,0:T(8,128)(2,1)}) %all-gather.5.cloned.1.call-update) | async-done | bytes 4194320 | tf_op jit(solution)/shard_map/all_gather | solution.py:11
  153.3 33.6 %fusion = f32[3,2048,1024]{2,1,0:T(8,128)} fusion(f32[3,2048]{1,0:T(4,128)S(1)} %exponential_multiply_fusion, f32[2048,2048]{0,1:T(8,128)} %copy.9, bf16[2048,1024]{1,0:T(8,128)(2,1)} %all-gather.5.cloned.1.call-done), kind=kOutput, calls=%fused_computation.1 | convolution fusion | flops 25794969600 | bytes 46161920 | tf_op jit(solution)/shard_map/trp,rq->tpq/dot_general | solution.py:16
Async XLA Ops:
  6.5 75.3 %all-gather.3.cloned.1.call-start = ((), (), s32[]{:S(2)}) async-start(), calls=%async_computation.2 | async-start | bytes 8912896 | tf_op jit(solution)/shard_map/all_gather | solution.py:13
  7.3 146.1 %all-gather.5.cloned.1.call-start = ((), (), s32[]{:S(2)}) async-start(), calls=%async_computation.3 | async-start | bytes 4718592 | tf_op jit(solution)/shard_map/all_gather | solution.py:11
Sparse Core Ops, SparseCore 0:
  8.9 72.8 all-gather.2
  84.2 69.0 all-gather.4
where the time goes:
time: 197 us; the launch traced here: 194 us
  waiting for transfers between devices  89.6 us (45%)
  blocking collectives  42 us (21%)
  matrix products  33.6 us (17%)
  local copies, waits for them, and re-layouts  13.7 us (7%)
  between operations  13.4 us (7%)
    all_gather x1, waiting for transfers between devices, on_device(): col_whole = lax.all_gather(col_block, 'row', axis=0, tiled=True)  58.4 us
    dot_general x1, matrix products, on_device(): jnp.einsum('trp,rq->tpq', weighted, col_whole, preferred_element_type=jnp...  33.6 us
    all_gather x1, waiting for transfers between devices, on_device(): lax.all_gather(pair_ints, 'col', axis=1, tiled=True).astype(jnp.float32)  30.5 us
    all_to_all x1, blocking collectives, on_device(): lax.all_to_all(pair_ints, ('row', 'col'), split_axis=0, concat_axis=1, ti...  23 us
    all_to_all x1, blocking collectives, on_device(): lax.all_to_all(pair_rows, 'col', split_axis=1, concat_axis=0, tiled=True)  18.9 us
    convert_element_type x1, local copies, waits for them, and re-layouts, on_device(): lax.all_gather(pair_ints, 'col', axis=1, tiled=True).astype(jnp.float32)  13 us
  transfers between devices with their start and end apart: 2, of which 2 were waited for; matrix products, arithmetic and copies ran while one was open for 8% of the time, Pallas kernels for 0%

commit v1 on v0

v1 whole, which is shorter than its diff:
```python
import jax
import jax.numpy as jnp
from jax import lax
from jax.experimental import pallas as pl
from jax.experimental.pallas import tpu as pltpu
from jax.sharding import PartitionSpec as P

NC, NG, SMAX, NT, NE = 8, 4, 5, 6, 27
TARGETS = ((0, 12), (0, 4), (4, 2), (0, 1), (0, 2), (1, 1), (3, 0), (3, 1), (1, 0), (4, 3))
PROGRAMS = (
    (
        (
            (0, 0, -1, 0, 0, ((0, 0, 0, 2), (1, 0, 0, 5), (2, 2, 0, 1), (3, 0, 0, 0)), 1),
            (0, 1, 0, 0, 1, (), 1),
            (0, 2, 1, 2, 0, ((1, 2, 1, 8),), 0),
            (0, 2, 2, 2, 1, ((2, 1, 1, 9), (4, 1, 1, 7)), 0),
            (0, 3, 3, 0, 12, ((5, 1, 12, 8), (1, 0, 12, 10), (3, 0, 12, 4)), 0),
            (0, 3, 4, 0, 2, ((1, 0, 2, 13), (3, 0, 2, 5)), 1),
            (0, 3, 5, 0, 4, ((6, 1, 4, 10), (4, 0, 4, 12), (0, 0, 4, 8), (3, 0, 4, 6)), 1),
            (1, 0, 7, 0, 3, (), 1),
            (1, 0, 8, 0, 5, (), 1),
            (1, 1, 9, 0, 14, ((5, 1, 14, 11), (3, 0, 14, 10)), 0),
            (1, 1, 10, 2, 2, ((2, 1, 5, 19), (4, 1, 5, 16)), 0),
            (1, 2, 11, 0, 6, ((3, 0, 6, 11),), 1),
            (1, 2, 12, 0, 8, ((3, 0, 8, 12),), 0),
            (1, 2, 14, 2, 3, ((2, 1, 4, 20), (4, 1, 4, 17)), 0),
            (1, 3, 15, 0, 7, (), 1),
            (2, 0, 17, 2, 4, ((4, 1, 0, 21),), 0),
            (2, 3, 19, 0, 10, ((7, 1, 10, 23), (3, 0, 10, 16)), 0),
            (3, 0, 20, 2, 5, ((2, 1, 3, 23),), 0),
        ),
        ((6, 0, 13), (13, 0, 15), (16, 0, 9), (18, 0, 11)),
    ),
    (
        (
            (0, 0, -1, 0, 1, ((0, 0, 1, 1), (1, 0, 1, 3), (5, 1, 1, 1), (3, 0, 1, 0)), 0),
            (0, 2, 1, 0, 13, ((4, 0, 13, 5), (3, 0, 13, 6)), 1),
            (0, 2, 2, 0, 3, ((1, 0, 3, 9), (0, 0, 3, 7), (7, 1, 3, 7), (3, 0, 3, 7)), 0),
            (0, 2, 3, 0, 5, ((5, 1, 5, 6), (7, 1, 5, 8), (3, 0, 5, 8)), 0),
            (1, 0, 4, 0, 12, (), 1),
            (1, 1, 7, 0, 15, ((6, 1, 15, 15), (0, 0, 15, 13), (3, 0, 15, 13)), 1),
            (1, 2, 8, 0, 9, ((8, 1, 9, 14), (3, 0, 9, 16)), 1),
            (1, 2, 9, 0, 7, ((3, 0, 7, 15),), 0),
            (1, 2, 10, 0, 14, (), 1),
            (1, 3, 12, 0, 8, (), 1),
            (2, 0, 13, 0, 11, ((6, 1, 11, 20), (8, 1, 11, 19), (3, 0, 11, 18)), 1),
            (2, 0, 14, 2, 0, ((0, 2, 2, 19),), 0),
            (2, 1, 15, 2, 1, ((2, 1, 14, 17),), 0),
            (3, 0, 16, 0, 10, (), 1),
        ),
        ((0, 0, 0), (5, 0, 2), (6, 0, 4), (11, 0, 6)),
    ),
    (
        (
            (0, 0, -1, 0, 2, ((2, 1, 2, 4), (4, 0, 2, 4), (0, 0, 2, 1), (1, 0, 2, 2), (3, 0, 2, 0)), 0),
            (0, 3, 2, 0, 14, ((9, 1, 14, 10), (1, 0, 14, 9), (3, 0, 14, 3)), 0),
            (0, 3, 3, 0, 6, ((8, 2, 3, 14), (3, 0, 6, 4)), 0),
            (1, 1, 6, 1, 7, ((6, 1, 7, 16),), 0),
            (1, 1, 7, 1, 1, ((6, 1, 1, 18),), 0),
            (1, 2, 8, 0, 12, ((5, 2, 1, 15), (3, 0, 12, 10)), 0),
            (1, 2, 9, 2, 0, ((1, 1, 7, 17),), 0),
            (1, 3, 12, 0, 4, ((0, 0, 4, 15), (2, 1, 4, 18), (3, 0, 4, 12)), 0),
            (1, 3, 14, 0, 10, ((4, 0, 10, 19), (3, 0, 10, 16)), 0),
            (2, 2, 18, 0, 8, ((9, 1, 8, 23), (3, 0, 8, 18)), 0),
            (2, 3, 22, 0, 0, ((3, 0, 0, 22),), 0),
        ),
        ((0, 0, 3), (1, 1, 3), (4, 0, 15), (5, 0, 7), (10, 0, 13), (11, 0, 11), (13, 0, 5), (15, 1, 2), (16, 1, 5), (17, 1, 4), (19, 0, 9), (20, 0, 1), (21, 1, 0), (23, 1, 6)),
    ),
    (
        (
            (0, 0, -1, 0, 3, ((0, 0, 3, 1), (1, 0, 3, 2), (5, 2, 1, 2), (4, 0, 3, 2), (3, 0, 3, 0)), 0),
            (0, 2, 1, 0, 15, ((4, 0, 15, 7), (1, 0, 15, 8), (3, 0, 15, 4)), 0),
            (0, 3, 2, 0, 7, ((5, 2, 2, 10), (4, 0, 7, 9), (3, 0, 7, 5)), 0),
            (1, 1, 5, 0, 13, ((3, 0, 13, 10),), 0),
            (1, 1, 6, 0, 11, ((2, 1, 11, 16), (3, 0, 11, 11)), 0),
            (1, 2, 7, 0, 5, ((9, 1, 5, 15), (0, 0, 5, 14), (3, 0, 5, 13)), 0),
            (1, 2, 8, 1, 14, ((6, 1, 14, 16),), 0),
            (1, 3, 9, 2, 0, ((1, 1, 14, 17),), 0),
            (2, 0, 11, 1, 12, ((6, 1, 12, 18),), 0),
            (2, 0, 13, 2, 1, ((0, 1, 12, 16),), 0),
            (2, 0, 14, 1, 11, ((6, 1, 11, 19),), 0),
            (2, 1, 15, 0, 9, ((3, 0, 9, 19),), 0),
            (2, 1, 17, 0, 1, ((7, 2, 3, 21), (5, 2, 5, 20), (3, 0, 1, 20)), 0),
            (3, 0, 21, 2, 2, ((0, 1, 15, 23),), 0),
        ),
        ((0, 0, 2), (3, 0, 14), (4, 0, 6), (10, 0, 12), (12, 0, 4), (16, 0, 10), (18, 0, 8), (19, 1, 9), (20, 1, 15), (22, 0, 0), (23, 1, 13), (24, 1, 10), (25, 1, 8)),
    ),
    (
        (
            (0, 0, -1, 0, 4, ((1, 0, 4, 5), (0, 0, 4, 1), (4, 0, 4, 3), (3, 0, 4, 0)), 0),
            (0, 2, 1, 2, 0, ((0, 1, 6, 8),), 0),
            (0, 3, 2, 0, 6, ((1, 0, 6, 11), (3, 0, 6, 4)), 0),
            (0, 3, 3, 0, 8, ((4, 0, 8, 12), (7, 2, 0, 9), (1, 0, 8, 12), (3, 0, 8, 5)), 0),
            (1, 0, 5, 0, 0, ((4, 0, 0, 15), (0, 0, 0, 15), (3, 0, 0, 7)), 0),
            (1, 1, 8, 2, 1, ((2, 1, 1, 12),), 0),
            (1, 1, 9, 2, 2, ((0, 1, 4, 17),), 0),
            (1, 2, 10, 0, 12, ((3, 0, 12, 10),), 0),
            (1, 3, 12, 0, 10, ((3, 0, 10, 15),), 0),
            (1, 3, 13, 0, 2, ((0, 0, 2, 20), (3, 0, 2, 14)), 0),
            (2, 0, 17, 0, 14, ((3, 0, 14, 17),), 0),
            (2, 1, 19, 1, 0, ((2, 2, 1, 20),), 0),
            (3, 0, 21, 2, 3, ((2, 1, 7, 22), (8, 2, 0, 20)), 0),
            (3, 3, 22, 1, 6, ((8, 1, 6, 24),), 0),
        ),
        ((0, 0, 5), (4, 0, 7), (6, 0, 9), (7, 0, 1), (11, 0, 13), (14, 0, 3), (15, 0, 11), (16, 1, 1), (18, 1, 7), (20, 0, 15), (23, 1, 3), (24, 1, 2), (25, 1, 5), (26, 1, 4)),
    ),
    (
        (
            (0, 0, -1, 0, 5, ((4, 0, 5, 3), (1, 0, 5, 3), (0, 0, 5, 1), (3, 0, 5, 0)), 0),
            (0, 2, 1, 0, 7, ((3, 0, 7, 4),), 0),
            (0, 2, 2, 0, 9, ((4, 0, 9, 9), (3, 0, 9, 6)), 0),
            (0, 3, 3, 0, 1, ((7, 2, 0, 9), (4, 0, 1, 11), (3, 0, 1, 7)), 0),
            (1, 1, 6, 0, 13, ((3, 0, 13, 11),), 0),
            (1, 1, 8, 0, 11, ((3, 0, 11, 15),), 0),
            (1, 1, 9, 0, 3, ((3, 0, 3, 14),), 0),
            (2, 0, 11, 1, 9, ((6, 1, 9, 20),), 0),
            (2, 0, 12, 2, 0, ((8, 2, 1, 19), (2, 1, 11, 18)), 0),
            (2, 0, 13, 0, 15, ((3, 0, 15, 20),), 0),
            (2, 1, 16, 1, 8, ((2, 2, 0, 20), (8, 1, 8, 21)), 0),
            (2, 3, 18, 1, 10, ((8, 1, 10, 22),), 0),
            (2, 3, 19, 1, 13, ((8, 1, 13, 24),), 0),
            (2, 3, 20, 1, 11, ((6, 1, 11, 23),), 0),
            (3, 1, 21, 1, 12, ((6, 1, 12, 24),), 0),
            (4, 1, 23, 1, 14, ((6, 1, 14, 25),), 0),
        ),
        ((0, 0, 4), (4, 0, 6), (5, 0, 8), (7, 0, 0), (10, 0, 12), (14, 0, 2), (15, 0, 10), (17, 0, 14), (22, 1, 15)),
    ),
    (
        (
            (0, 0, -1, 0, 6, ((1, 0, 6, 3), (0, 0, 6, 3), (4, 0, 6, 2), (3, 0, 6, 0)), 0),
            (0, 3, 1, 0, 10, ((9, 2, 0, 6), (3, 0, 10, 4)), 0),
            (0, 3, 2, 0, 2, ((3, 0, 2, 6),), 0),
            (0, 3, 3, 0, 4, ((3, 0, 4, 5),), 0),
            (1, 2, 9, 0, 14, ((3, 0, 14, 12),), 0),
            (1, 2, 10, 1, 2, ((8, 1, 2, 19), (2, 2, 0, 15)), 0),
            (1, 3, 12, 0, 8, ((1, 0, 8, 18), (3, 0, 8, 13)), 0),
            (2, 0, 15, 0, 0, ((0, 0, 0, 16), (1, 0, 0, 22), (3, 0, 0, 16)), 0),
            (2, 1, 16, 0, 12, ((3, 0, 12, 18),), 0),
            (3, 3, 20, 2, 0, ((2, 1, 5, 24), (4, 1, 5, 25)), 0),
            (3, 3, 22, 2, 1, ((4, 1, 2, 24),), 0),
        ),
        ((0, 0, 7), (4, 0, 11), (5, 0, 5), (6, 0, 3), (7, 1, 5), (8, 1, 3), (11, 0, 15), (13, 0, 9), (14, 0, 1), (17, 1, 7), (18, 0, 13), (19, 1, 1), (21, 1, 6), (23, 1, 0), (24, 1, 4)),
    ),
    (
        (
            (0, 0, -1, 0, 7, ((7, 2, 0, 1), (1, 0, 7, 2), (0, 0, 7, 5), (4, 0, 7, 1), (3, 0, 7, 0)), 0),
            (0, 2, 1, 0, 11, ((1, 0, 11, 6), (3, 0, 11, 4)), 0),
            (0, 3, 2, 0, 3, ((0, 0, 3, 13), (3, 0, 3, 6)), 0),
            (0, 3, 3, 0, 5, ((1, 0, 5, 7), (0, 0, 5, 11), (3, 0, 5, 5)), 0),
            (1, 1, 7, 1, 11, ((4, 2, 0, 12), (8, 1, 11, 11)), 0),
            (1, 1, 8, 0, 15, ((4, 0, 15, 13), (3, 0, 15, 11)), 0),
            (1, 1, 9, 0, 9, ((2, 2, 1, 13), (3, 0, 9, 13)), 0),
            (1, 2, 10, 2, 0, ((6, 2, 0, 14),), 0),
            (1, 2, 11, 0, 1, ((3, 0, 1, 14),), 0),
            (2, 0, 14, 0, 13, ((3, 0, 13, 18),), 0),
            (2, 0, 15, 1, 9, ((8, 1, 9, 20),), 0),
            (2, 2, 17, 1, 14, ((8, 1, 14, 21),), 0),
            (2, 3, 19, 2, 1, ((2, 1, 9, 20),), 0),
            (2, 3, 20, 1, 13, ((8, 1, 13, 22),), 0),
            (3, 2, 23, 1, 12, ((8, 1, 12, 23),), 0),
        ),
        ((0, 0, 6), (4, 0, 10), (5, 0, 4), (6, 0, 2), (12, 0, 14), (13, 0, 8), (16, 0, 0), (18, 0, 12), (21, 1, 10), (22, 1, 8), (24, 1, 15)),
    ),
    (
        (
            (0, 0, -1, 0, 8, ((0, 0, 8, 3), (4, 0, 8, 1), (1, 0, 8, 3), (3, 0, 8, 0)), 0),
            (0, 3, 1, 0, 4, ((4, 0, 4, 7), (3, 0, 4, 5)), 0),
            (0, 3, 2, 0, 12, ((3, 0, 12, 6),), 0),
            (0, 3, 3, 0, 10, ((1, 0, 10, 11), (0, 0, 10, 12), (3, 0, 10, 7)), 0),
            (1, 1, 7, 2, 0, ((2, 2, 1, 13),), 0),
            (1, 1, 8, 1, 6, ((8, 1, 6, 13), (6, 1, 6, 13)), 0),
            (1, 2, 9, 0, 14, ((0, 0, 14, 17), (3, 0, 14, 12)), 0),
            (1, 2, 10, 1, 7, ((6, 1, 7, 14), (8, 1, 7, 14)), 0),
            (1, 3, 12, 0, 6, ((1, 0, 6, 16), (3, 0, 6, 14)), 0),
            (1, 3, 15, 0, 0, ((3, 0, 0, 16),), 0),
            (2, 0, 16, 1, 2, ((6, 1, 2, 17),), 0),
            (2, 1, 18, 1, 3, ((6, 1, 3, 19),), 0),
            (2, 1, 19, 2, 1, ((2, 2, 2, 21),), 0),
            (2, 2, 20, 0, 2, ((3, 0, 2, 20),), 0),
            (3, 0, 22, 1, 0, ((8, 1, 0, 19), (6, 1, 0, 21)), 0),
            (3, 0, 23, 1, 1, ((8, 1, 1, 20), (6, 1, 1, 22)), 0),
        ),
        ((0, 0, 9), (4, 0, 5), (5, 0, 13), (6, 0, 11), (11, 0, 15), (13, 0, 7), (14, 0, 1), (17, 1, 4), (21, 0, 3), (24, 1, 5)),
    ),
    (
        (
            (0, 0, -1, 0, 9, ((0, 0, 9, 2), (1, 0, 9, 2), (4, 0, 9, 2), (3, 0, 9, 0)), 0),
            (0, 2, 1, 0, 5, ((1, 0, 5, 6), (3, 0, 5, 4)), 0),
            (0, 2, 2, 0, 13, ((4, 0, 13, 10), (0, 0, 13, 6), (3, 0, 13, 5)), 0),
            (0, 3, 3, 0, 11, ((1, 0, 11, 8), (0, 0, 11, 8), (3, 0, 11, 6)), 0),
            (0, 3, 4, 1, 11, ((8, 1, 11, 12),), 0),
            (1, 1, 8, 2, 0, ((2, 1, 11, 15), (4, 1, 11, 17)), 0),
            (1, 1, 9, 0, 15, ((3, 0, 15, 11),), 0),
            (1, 1, 10, 0, 7, ((3, 0, 7, 13),), 0),
            (1, 1, 11, 0, 1, ((3, 0, 1, 14),), 0),
            (2, 1, 15, 1, 12, ((8, 1, 12, 21),), 0),
            (2, 1, 17, 0, 3, ((3, 0, 3, 21),), 0),
            (3, 3, 22, 2, 1, ((2, 1, 15, 23),), 0),
        ),
        ((0, 0, 8), (5, 0, 4), (6, 0, 12), (7, 0, 10), (12, 0, 14), (13, 1, 10), (14, 0, 6), (16, 0, 0), (18, 1, 13), (19, 1, 14), (20, 0, 2), (21, 1, 15), (23, 1, 8), (24, 1, 9)),
    ),
    (
        (
            (0, 0, -1, 0, 10, ((0, 0, 10, 1), (1, 0, 10, 3), (4, 0, 10, 3), (3, 0, 10, 0)), 0),
            (0, 3, 1, 0, 8, ((1, 0, 8, 7), (3, 0, 8, 6)), 0),
            (0, 3, 2, 0, 14, ((3, 0, 14, 7),), 0),
            (0, 3, 3, 0, 6, ((4, 0, 6, 12), (1, 0, 6, 12), (3, 0, 6, 8)), 0),
            (1, 2, 7, 0, 4, ((3, 0, 4, 14),), 0),
            (1, 2, 8, 0, 12, ((0, 0, 12, 16), (3, 0, 12, 15)), 0),
            (1, 2, 9, 0, 2, ((3, 0, 2, 16),), 0),
            (2, 0, 13, 1, 4, ((6, 1, 4, 17),), 0),
            (2, 3, 16, 0, 0, ((3, 0, 0, 22),), 0),
            (3, 0, 17, 1, 7, ((8, 1, 7, 24),), 0),
            (3, 1, 18, 2, 0, ((0, 1, 0, 23),), 0),
            (3, 3, 19, 1, 2, ((6, 1, 2, 23),), 0),
            (3, 3, 20, 1, 3, ((6, 1, 3, 24),), 0),
        ),
        ((0, 0, 11), (4, 0, 9), (5, 0, 15), (6, 0, 7), (10, 0, 13), (11, 0, 5), (12, 0, 3), (14, 1, 5), (15, 0, 1), (21, 1, 6), (22, 1, 0), (23, 1, 1)),
    ),
    (
        (
            (0, 0, -1, 0, 11, ((0, 0, 11, 1), (4, 0, 11, 3), (1, 0, 11, 3), (3, 0, 11, 0)), 0),
            (0, 2, 1, 2, 0, ((8, 2, 0, 8),), 0),
            (0, 2, 2, 0, 9, ((1, 0, 9, 6), (3, 0, 9, 4)), 0),
            (0, 2, 3, 2, 1, ((0, 1, 11, 7),), 0),
            (0, 2, 4, 0, 15, ((4, 0, 15, 9), (3, 0, 15, 5)), 0),
            (0, 2, 5, 0, 7, ((1, 0, 7, 9), (4, 0, 7, 10), (3, 0, 7, 6)), 0),
            (1, 1, 9, 1, 8, ((8, 1, 8, 13),), 0),
            (1, 1, 10, 0, 13, ((0, 0, 13, 14), (3, 0, 13, 10)), 0),
            (1, 1, 11, 0, 5, ((3, 0, 5, 11),), 0),
            (1, 1, 12, 1, 9, ((6, 1, 9, 12), (2, 2, 4, 17)), 0),
            (1, 2, 13, 0, 3, ((4, 0, 3, 17), (3, 0, 3, 12)), 0),
            (2, 0, 18, 0, 1, ((3, 0, 1, 15),), 0),
            (2, 0, 19, 1, 12, ((8, 1, 12, 19),), 0),
            (2, 1, 20, 1, 13, ((6, 1, 13, 20), (8, 1, 13, 21)), 0),
            (3, 0, 21, 1, 14, ((6, 1, 14, 22),), 0),
        ),
        ((0, 0, 10), (6, 0, 8), (7, 0, 14), (8, 0, 6), (14, 0, 4), (15, 0, 12), (16, 0, 2), (17, 1, 11), (22, 0, 0), (23, 1, 10), (24, 1, 15)),
    ),
    (
        (
            (0, 0, -1, 0, 12, ((0, 0, 12, 3), (4, 0, 12, 2), (1, 0, 12, 2), (3, 0, 12, 0)), 0),
            (0, 2, 1, 0, 14, ((0, 0, 14, 9), (1, 0, 14, 9), (3, 0, 14, 3)), 0),
            (0, 3, 2, 0, 0, ((4, 0, 0, 9), (2, 2, 0, 10), (3, 0, 0, 4)), 0),
            (0, 3, 3, 0, 8, ((3, 0, 8, 5),), 0),
            (1, 2, 6, 2, 0, ((1, 1, 3, 18),), 0),
            (1, 2, 7, 0, 2, ((3, 0, 2, 9),), 0),
            (1, 2, 8, 0, 4, ((3, 0, 4, 10),), 0),
            (1, 3, 11, 0, 10, ((3, 0, 10, 11),), 0),
            (2, 0, 13, 2, 1, ((1, 1, 0, 22),), 0),
            (2, 2, 16, 0, 6, ((6, 2, 0, 18), (3, 0, 6, 18)), 0),
            (3, 2, 19, 1, 6, ((6, 1, 6, 22),), 0),
            (3, 2, 20, 1, 0, ((6, 1, 0, 21),), 0),
            (3, 3, 21, 1, 7, ((6, 1, 7, 23),), 0),
            (4, 0, 22, 1, 1, ((8, 1, 1, 23),), 0),
        ),
        ((0, 0, 13), (4, 0, 1), (5, 0, 9), (9, 0, 5), (10, 0, 3), (12, 0, 11), (14, 0, 15), (15, 0, 7), (17, 1, 2), (18, 1, 3), (23, 1, 4), (24, 1, 5)),
    ),
    (
        (
            (0, 0, -1, 0, 13, ((6, 2, 1, 3), (1, 0, 13, 2), (4, 0, 13, 2), (0, 0, 13, 1), (3, 0, 13, 0)), 0),
            (0, 2, 1, 0, 1, ((4, 0, 1, 8), (1, 0, 1, 11), (3, 0, 1, 4)), 0),
            (0, 3, 2, 0, 9, ((0, 0, 9, 8), (3, 0, 9, 5)), 0),
            (1, 1, 6, 0, 5, ((3, 0, 5, 9),), 0),
            (1, 1, 7, 0, 3, ((3, 0, 3, 10),), 0),
            (1, 2, 8, 0, 11, ((0, 0, 11, 13), (3, 0, 11, 12)), 0),
            (2, 0, 12, 1, 15, ((4, 2, 0, 18), (8, 1, 15, 17)), 0),
            (2, 1, 13, 0, 15, ((3, 0, 15, 14),), 0),
            (2, 1, 14, 0, 7, ((3, 0, 7, 15),), 0),
            (2, 1, 15, 2, 0, ((4, 1, 11, 19),), 0),
            (2, 3, 16, 2, 1, ((8, 2, 2, 21), (2, 1, 8, 19)), 0),
            (3, 0, 19, 2, 2, ((8, 2, 3, 24), (2, 1, 15, 21)), 0),
            (3, 0, 20, 1, 11, ((2, 2, 1, 22), (8, 1, 11, 25)), 0),
            (3, 3, 22, 1, 8, ((8, 1, 8, 26),), 0),
            (3, 3, 23, 1, 9, ((6, 1, 9, 24),), 0),
        ),
        ((0, 0, 12), (3, 0, 14), (4, 0, 0), (5, 0, 8), (9, 0, 2), (10, 0, 4), (11, 0, 10), (17, 1, 10), (18, 0, 6), (21, 1, 14), (24, 1, 12), (25, 1, 13)),
    ),
    (
        (
            (0, 0, -1, 0, 14, ((4, 0, 14, 1), (0, 0, 14, 2), (1, 0, 14, 2), (3, 0, 14, 0)), 0),
            (0, 3, 1, 0, 2, ((1, 0, 2, 9), (4, 0, 2, 7), (3, 0, 2, 5)), 0),
            (0, 3, 2, 0, 12, ((0, 0, 12, 8), (1, 0, 12, 8), (3, 0, 12, 4)), 0),
            (1, 0, 3, 0, 10, ((0, 0, 10, 14), (3, 0, 10, 7)), 0),
            (1, 2, 7, 0, 8, ((3, 0, 8, 10),), 0),
            (1, 2, 9, 0, 0, ((6, 2, 1, 19), (3, 0, 0, 11)), 0),
            (1, 3, 12, 0, 6, ((3, 0, 6, 13),), 0),
            (2, 1, 14, 1, 1, ((8, 1, 1, 18),), 0),
            (2, 2, 15, 0, 4, ((3, 0, 4, 15),), 0),
            (2, 3, 17, 1, 4, ((8, 1, 4, 19),), 0),
            (3, 0, 19, 1, 5, ((8, 1, 5, 21),), 0),
            (3, 1, 20, 2, 0, ((4, 1, 1, 22),), 0),
        ),
        ((0, 0, 15), (4, 0, 13), (5, 0, 3), (6, 0, 11), (8, 0, 9), (10, 0, 1), (11, 0, 7), (13, 1, 0), (16, 0, 5), (18, 1, 2), (21, 1, 6), (22, 1, 7), (23, 1, 3)),
    ),
    (
        (
            (0, 0, -1, 0, 15, ((0, 0, 15, 1), (2, 2, 0, 1), (1, 0, 15, 4), (3, 0, 15, 0)), 0),
            (0, 2, 1, 0, 3, ((7, 2, 0, 7), (3, 0, 3, 5)), 0),
            (0, 2, 2, 0, 13, ((2, 2, 2, 9), (3, 0, 13, 4)), 0),
            (0, 3, 3, 0, 11, ((3, 0, 11, 6),), 0),
            (1, 1, 6, 0, 9, ((0, 0, 9, 15), (3, 0, 9, 8)), 0),
            (1, 1, 8, 0, 1, ((0, 0, 1, 17), (1, 0, 1, 18), (3, 0, 1, 10)), 0),
            (1, 2, 9, 0, 7, ((4, 0, 7, 14), (3, 0, 7, 11)), 0),
            (2, 0, 12, 1, 8, ((4, 2, 1, 16), (8, 1, 8, 17)), 0),
            (2, 1, 14, 0, 5, ((3, 0, 5, 16),), 0),
            (3, 0, 16, 1, 12, ((8, 1, 12, 21),), 0),
            (3, 0, 18, 2, 0, ((2, 1, 15, 22),), 0),
            (3, 0, 20, 2, 1, ((6, 2, 1, 22), (4, 1, 9, 23)), 0),
            (3, 2, 21, 2, 2, ((2, 1, 10, 23),), 0),
            (3, 3, 22, 1, 14, ((6, 1, 14, 23),), 0),
            (3, 3, 23, 1, 15, ((6, 1, 15, 24), (8, 1, 15, 25)), 0),
            (3, 3, 24, 2, 3, ((2, 1, 13, 26),), 0),
        ),
        ((0, 0, 14), (4, 0, 12), (5, 0, 2), (7, 0, 10), (10, 0, 8), (11, 0, 0), (13, 0, 6), (15, 0, 4), (17, 1, 13), (19, 1, 11), (25, 1, 9), (26, 1, 10)),
    ),
)
VMEM_LIMIT = 24 << 20

F32, BF16 = jnp.float32, jnp.bfloat16
MESH = pl.DeviceIdType.MESH
NT_PTS = 3
PAIRS, ROWS, COLS, OWN = 2048, 2048, 1024, 128
KC = PAIRS // NC
KK = 512
NK = PAIRS // KK
PER = KK // KC
MB, NB = 256, 256
NM = ROWS // MB
START = SMAX + PER
STEPS = NC + SMAX


def flip(value, bits):
    return [jnp.int32(b) * (1 - 2 * ((value // b) % 2)) for b in bits]


def flipped(value, deltas, bits, mask):
    for delta, bit in zip(deltas, bits):
        if mask & bit:
            value = value + delta
    return value


def weigh(x, factor, w_ref):
    x = x.astype(F32)
    for t in range(NT_PTS):
        w_ref[pl.ds(t * MB, MB), :] = (x * factor(t)).astype(BF16)


def product(w, y):
    return lax.dot_general(w, y, (((1,), (1,)), ((), ())), preferred_element_type=F32)


def gather_kernel(points, weights, own_ref, den_ref, acc, x_ref, y_ref, f_ref,
                  transit, w_ref, send_sem, recv_sem, local_sem):
    row, col = lax.axis_index("row"), lax.axis_index("col")
    row_d, col_d = flip(row, (1, 2, 4)), flip(col, (1, 2, 4, 8))
    peers = [
        {"row": flipped(row, row_d, (1, 2, 4), dr), "col": flipped(col, col_d, (1, 2, 4, 8), dc)}
        for dr, dc in TARGETS
    ]
    barrier = pltpu.get_barrier_semaphore()
    for peer in peers:
        pl.semaphore_signal(barrier, inc=1, device_id=peer, device_id_type=MESH)

    high = row // 4
    code = row * 2 + high
    code_d = flip(code, (1, 2, 4, 8))

    def lanes(j):
        return pl.ds(pl.multiple_of((j % PER) * KC, KC), KC)

    def place(kind, mark, j):
        if kind == 2:
            return transit.at[j, mark]
        slot = flipped(code, code_d, (1, 2, 4, 8), mark)
        if kind == 0:
            return x_ref.at[j // PER, pl.ds(pl.multiple_of(slot * OWN, OWN), OWN), lanes(j)]
        slot = slot % 8
        return y_ref.at[j // PER, pl.ds(pl.multiple_of(slot * OWN, OWN), OWN), lanes(j)]

    for k in range(NK):
        x_ref[k, pl.ds(pl.multiple_of(col * OWN, OWN), OWN), :] = own_ref[pl.ds(k * KK, KK), :].T
    for t in range(NT_PTS):
        f_ref[t] = weights[t] * jnp.exp(-points[t] * den_ref[...])
    pl.semaphore_wait(barrier, len(TARGETS))

    k_col = col // 2
    bits = [((row // b) % 2 + (k_col // b) % 2) % 2 for b in (4, 2, 1)]
    which = (bits[0] * 4 + bits[1] * 2 + bits[2]) * 2 + ((col % 2) + high) % 2

    def arrived(kind, mark, event, j):
        ref = place(kind, mark, j)
        pltpu.make_async_copy(ref, ref, recv_sem.at[j, event]).wait()

    def act(action, j):
        _, _, event, kind, mark, kids, local = action
        if event >= 0:
            arrived(kind, mark, event, j)
        src = place(kind, mark, j)
        for target, to_kind, to_mark, to_event in kids:
            pltpu.make_async_remote_copy(
                src_ref=src, dst_ref=place(to_kind, to_mark, j),
                send_sem=send_sem.at[j], recv_sem=recv_sem.at[j, to_event],
                device_id=peers[target], device_id_type=MESH,
            ).start()
        if local:
            pltpu.make_async_copy(src, place(1, mark, j), local_sem.at[j]).start()

    def bulk_wait(sem, copies):
        ref = acc.at[0, pl.ds(0, copies * OWN * KC // (2 * COLS)), :]
        pltpu.make_async_copy(ref, ref, sem).wait()

    def settle(j):
        for g, (actions, last) in enumerate(PROGRAMS):
            @pl.when(which == g)
            def _():
                for event, kind, mark in last:
                    arrived(kind, mark, event, j)
                copies = sum(a[6] for a in actions)
                if copies:
                    bulk_wait(local_sem.at[j], copies)

    def block(k, m, first):
        rows = pl.ds(pl.multiple_of(m * MB, MB), MB)
        weigh(x_ref[k, rows, :], lambda t: f_ref[t, pl.ds(k, 1), :], w_ref)

        @pl.loop(0, COLS // NB)
        def _(n):
            at = pl.ds(pl.multiple_of(n * NB, NB), NB)
            d = product(w_ref[...], y_ref[k, at, :])
            for t in range(NT_PTS):
                if first:
                    acc[t, rows, at] = d[t * MB:(t + 1) * MB]
                else:
                    acc[t, rows, at] += d[t * MB:(t + 1) * MB]

    @pl.loop(0, STEPS)
    def _(p):
        k = jnp.maximum(p - START, 0) // PER
        part = jnp.maximum(p - START, 0) % PER
        busy = p >= START

        @pl.when(jnp.logical_and(busy, part == 0))
        def _():
            for i in range(PER):
                settle(k * PER + i)

        for group in range(NG):
            for g, (actions, _last) in enumerate(PROGRAMS):
                mine = [a for a in actions if a[1] == group]
                if mine:
                    @pl.when(which == g)
                    def _():
                        for lag in sorted({a[0] for a in mine}):
                            @pl.when(jnp.logical_and(p >= lag, p < NC + lag))
                            def _():
                                for a in mine:
                                    if a[0] == lag:
                                        act(a, p - lag)

            blocks = NM // PER // NG
            for b in range(blocks):
                m = part * (NM // PER) + group * blocks + b

                @pl.when(jnp.logical_and(busy, k == 0))
                def _():
                    block(0, m, True)

                @pl.when(jnp.logical_and(busy, k > 0))
                def _():
                    block(k, m, False)

    for i in range(PER):
        settle(NC - PER + i)
    for g, (actions, _last) in enumerate(PROGRAMS):
        @pl.when(which == g)
        def _():
            @pl.loop(0, NC)
            def _(j):
                bulk_wait(send_sem.at[j], sum(len(a[5]) for a in actions))


def last_kernel(acc, x_ref, y_ref, f_ref, out, w_ref, buf, sem):
    def copy(m, slot):
        return pltpu.make_async_copy(
            buf.at[slot], out.at[:, pl.ds(pl.multiple_of(m * MB, MB), MB), :], sem.at[slot]
        )

    @pl.loop(0, NM)
    def _(m):
        slot = m % 2
        rows = pl.ds(pl.multiple_of(m * MB, MB), MB)
        weigh(x_ref[NK - 1, rows, :], lambda t: f_ref[t, NK - 1:NK, :], w_ref)

        @pl.when(m >= 2)
        def _():
            copy(m - 2, slot).wait()

        @pl.loop(0, COLS // NB)
        def _(n):
            at = pl.ds(pl.multiple_of(n * NB, NB), NB)
            d = product(w_ref[...], y_ref[NK - 1, at, :])
            for t in range(NT_PTS):
                buf[slot, t, :, at] = acc[t, rows, at] + d[t * MB:(t + 1) * MB]

        copy(m, slot).start()

    copy(NM - 2, 0).wait()
    copy(NM - 1, 1).wait()


def on_device(pair_ints, denominators, lap_points, lap_weights):
    vmem = pl.BlockSpec(memory_space=pltpu.VMEM)
    smem = pl.BlockSpec(memory_space=pltpu.SMEM)
    held = pl.pallas_call(
        gather_kernel,
        out_shape=(
            pltpu.VMEM((NT_PTS, ROWS, COLS), F32),
            pltpu.VMEM((NK, ROWS, KK), BF16),
            pltpu.VMEM((NK, COLS, KK), BF16),
            pltpu.VMEM((NT_PTS, NK, KK), F32),
        ),
        in_specs=[smem, smem, vmem, vmem],
        out_specs=(vmem,) * 4,
        scratch_shapes=[
            pltpu.VMEM((NC, NT, OWN, KC), BF16),
            pltpu.VMEM((NT_PTS * MB, KK), BF16),
            pltpu.SemaphoreType.DMA((NC,)),
            pltpu.SemaphoreType.DMA((NC, NE)),
            pltpu.SemaphoreType.DMA((NC,)),
        ],
        compiler_params=pltpu.CompilerParams(
            collective_id=0, has_side_effects=True, vmem_limit_bytes=VMEM_LIMIT
        ),
    )(lap_points, lap_weights, pair_ints, denominators.reshape(NK, KK))
    held = [pltpu.with_memory_space_constraint(a, pltpu.VMEM) for a in held]
    return pl.pallas_call(
        last_kernel,
        out_shape=jax.ShapeDtypeStruct((NT_PTS, ROWS, COLS), F32),
        in_specs=[vmem] * 4,
        out_specs=pl.BlockSpec(memory_space=pl.ANY),
        scratch_shapes=[
            pltpu.VMEM((NT_PTS * MB, KK), BF16),
            pltpu.VMEM((2, NT_PTS, MB, COLS), F32),
            pltpu.SemaphoreType.DMA((2,)),
        ],
        compiler_params=pltpu.CompilerParams(vmem_limit_bytes=VMEM_LIMIT),
    )(*held)


def solution(mesh):
    in_specs = (P(None, ("row", "col")), P(), P(), P())
    out_specs = P(None, "row", "col")
    return jax.shard_map(
        on_device, mesh=mesh, in_specs=in_specs, out_specs=out_specs, check_vma=False
    )
```

time: 197 us -> 115 us (0.58); the launches traced: 194 us -> 114 us
  Pallas kernels: 0 us -> 113 us
  waiting for transfers between devices: 89.6 us -> 0 us
  blocking collectives: 42 us -> 0 us
  matrix products: 33.6 us -> 0 us
  between operations: 13.4 us -> 0.01 us
  local copies, waits for them, and re-layouts: 13.7 us -> 1.3 us
    pallas_call x0 -> x2, Pallas kernels: none -> 113 us  [the longest x1 97.9 us: on_device(): pl.pallas_call(gather_kernel, out_shape=(pltpu.VMEM((NT_PTS, ROWS, COLS),...]
    all_gather x2 -> x0, waiting for transfers between devices: 88.9 us -> none  [the longest x1 58.4 us: on_device(): col_whole = lax.all_gather(col_block, 'row', axis=0, tiled=True)]
    all_to_all x2 -> x0, blocking collectives: 42 us -> none  [the longest x1 23 us: on_device(): lax.all_to_all(pair_ints, ('row', 'col'), split_axis=0, concat_axis=1, ti...]
    dot_general x1 -> x0, matrix products: 33.6 us -> none  [on_device(): jnp.einsum('trp,rq->tpq', weighted, col_whole, preferred_element_type=jnp...]
    convert_element_type x1 -> x0, local copies, waits for them, and re-layouts: 13 us -> none  [on_device(): lax.all_gather(pair_ints, 'col', axis=1, tiled=True).astype(jnp.float32)]
  transfers between devices with their start and end apart: 2 -> 0, of which waited for: 2 -> 0; matrix products, arithmetic and copies ran while one was open for 8% -> 0% of each run, Pallas kernels for 0% -> 0%
where the time goes in v1:
time: 115 us; the launch traced here: 114 us
  Pallas kernels  113 us (98%)
  local copies, waits for them, and re-layouts  1.3 us (1%)
    pallas_call x1, Pallas kernels, on_device(): pl.pallas_call(gather_kernel, out_shape=(pltpu.VMEM((NT_PTS, ROWS, COLS),...  97.9 us
    pallas_call x1, Pallas kernels, on_device(): pl.pallas_call(last_kernel, out_shape=jax.ShapeDtypeStruct((NT_PTS, ROWS,...  15.2 us

profile of v1, /device:TPU:36, one launch (start us, length us, event | category | flops | bytes accessed | tf_op | source)
XLA Modules:
  0.0 114.4 jit_solution(5726044541383690001)
XLA Ops:
  0.0 1.3 %reshape.3.den_ref = f32[4,512]{1,0:T(4,128)} reshape(f32[2048]{0:T(1024)} %param.5) | data formatting | bytes 16384 | tf_op jit(solution)/shard_map/reshape | solution.py:537
  1.3 97.9 %shard_map.46 = (f32[3,2048,1024]{2,1,0:T(8,128)S(1)}, bf16[4,2048,512]{2,1,0:T(8,128)(2,1)S(1)}, bf16[4,1024,512]{2,1,0:T(8,128)(2,1)S(1)}, f32[3,4,512]{2,1,0:T(4,128)S(1)}) custom-call(f32[3]{0:T(128)} %points.1, f32[3]{0:T(128)} %weights.1, bf16[2048,128]{1,0:T(8,128)(2,1)} %own_ref.1, f32[4,512]{1,0:T(4,128)} %reshape.3.den_ref), custom_call_target="tpu_custom_call" | custom-call | tf_op jit(solution)/shard_map/pallas_call | solution.py:517
  99.2 15.2 %shard_map.47 = f32[3,2048,1024]{2,1,0:T(8,128)} custom-call(f32[3,2048,1024]{2,1,0:T(8,128)S(1)} %get-tuple-element.9.acc, bf16[4,2048,512]{2,1,0:T(8,128)(2,1)S(1)} %get-tuple-element.10.x_ref, bf16[4,1024,512]{2,1,0:T(8,128)(2,1)S(1)} %get-tuple-element.11.y_ref, f32[3,4,512]{2,1,0:T(4,128)S(1)} %get-tuple-element.12.f_ref), custom_call_target="tpu_custom_call" | custom-call | tf_op jit(solution)/shard_map/pallas_call | solution.py:539

commit v2 on v0

v2 whole, which is shorter than its diff:
```python
import jax
import jax.numpy as jnp
from jax import lax
from jax.experimental import pallas as pl
from jax.experimental.pallas import tpu as pltpu
from jax.sharding import PartitionSpec as P

NC, NG, SMAX, NT, NE = 8, 4, 7, 6, 27
TARGETS = ((0, 12), (0, 4), (4, 2), (0, 1), (0, 2), (3, 0), (1, 1), (3, 1), (1, 0), (4, 3))
PROGRAMS = (
    (
        (
            (0, 0, -1, 0, 0, ((0, 0, 0, 3), (1, 0, 0, 4), (2, 2, 1, 5), (3, 0, 0, 0)), 1),
            (0, 1, 0, 0, 1, (), 1),
            (0, 3, 1, 2, 0, ((1, 2, 1, 8),), 0),
            (0, 3, 2, 2, 1, ((2, 1, 1, 9), (4, 1, 1, 7)), 0),
            (1, 0, 3, 0, 4, ((5, 1, 4, 9), (4, 0, 4, 8), (0, 0, 4, 7), (3, 0, 4, 4)), 1),
            (1, 0, 4, 0, 2, ((1, 0, 2, 12), (3, 0, 2, 5)), 1),
            (1, 0, 5, 0, 12, ((6, 1, 12, 8), (1, 0, 12, 10), (3, 0, 12, 6)), 0),
            (1, 1, 6, 0, 5, (), 1),
            (1, 1, 7, 0, 3, (), 1),
            (2, 0, 9, 2, 2, ((2, 1, 5, 17), (4, 1, 5, 16)), 0),
            (2, 0, 10, 0, 14, ((6, 1, 14, 16), (3, 0, 14, 10)), 0),
            (2, 1, 11, 0, 8, ((3, 0, 8, 11),), 0),
            (2, 1, 12, 2, 3, ((2, 1, 4, 20), (4, 1, 4, 17)), 0),
            (2, 1, 13, 0, 6, ((3, 0, 6, 12),), 1),
            (2, 2, 16, 0, 7, (), 1),
            (3, 0, 17, 2, 4, ((4, 1, 0, 22),), 0),
            (3, 2, 18, 0, 10, ((7, 1, 10, 22), (3, 0, 10, 16)), 0),
            (4, 2, 20, 2, 5, ((2, 1, 3, 23),), 0),
        ),
        ((8, 0, 13), (14, 0, 9), (15, 0, 15), (19, 0, 11)),
    ),
    (
        (
            (0, 0, -1, 0, 1, ((0, 0, 1, 2), (1, 0, 1, 3), (6, 1, 1, 1), (3, 0, 1, 0)), 0),
            (0, 3, 1, 0, 5, ((6, 1, 5, 6), (7, 1, 5, 7), (3, 0, 5, 6)), 0),
            (1, 0, 2, 0, 3, ((1, 0, 3, 8), (0, 0, 3, 6), (7, 1, 3, 8), (3, 0, 3, 7)), 0),
            (1, 0, 3, 0, 13, ((4, 0, 13, 5), (3, 0, 13, 8)), 1),
            (1, 2, 6, 0, 12, (), 1),
            (2, 0, 7, 0, 9, ((8, 1, 9, 14), (3, 0, 9, 14)), 1),
            (2, 1, 8, 0, 7, ((3, 0, 7, 16),), 0),
            (2, 1, 9, 0, 15, ((5, 1, 15, 16), (0, 0, 15, 15), (3, 0, 15, 15)), 1),
            (2, 2, 10, 0, 14, (), 1),
            (2, 3, 11, 0, 8, (), 1),
            (3, 1, 13, 2, 0, ((0, 2, 2, 20),), 0),
            (3, 1, 14, 2, 1, ((2, 1, 14, 17),), 0),
            (3, 2, 15, 0, 11, ((5, 1, 11, 20), (8, 1, 11, 22), (3, 0, 11, 19)), 1),
            (4, 0, 16, 0, 10, (), 1),
        ),
        ((0, 0, 0), (4, 0, 4), (5, 0, 2), (12, 0, 6)),
    ),
    (
        (
            (0, 0, -1, 0, 2, ((2, 1, 2, 1), (4, 0, 2, 4), (0, 0, 2, 2), (1, 0, 2, 2), (3, 0, 2, 0)), 0),
            (1, 0, 2, 0, 6, ((8, 2, 3, 12), (3, 0, 6, 3)), 0),
            (1, 0, 3, 0, 14, ((9, 1, 14, 10), (1, 0, 14, 10), (3, 0, 14, 4)), 0),
            (1, 3, 6, 1, 7, ((5, 1, 7, 16),), 0),
            (2, 0, 7, 1, 1, ((5, 1, 1, 18),), 0),
            (2, 1, 8, 0, 4, ((0, 0, 4, 13), (2, 1, 4, 16), (3, 0, 4, 10)), 0),
            (2, 1, 9, 2, 0, ((1, 1, 7, 17),), 0),
            (2, 1, 10, 0, 12, ((6, 2, 1, 14), (3, 0, 12, 11)), 0),
            (2, 2, 11, 0, 10, ((4, 0, 10, 18), (3, 0, 10, 12)), 0),
            (3, 3, 18, 0, 0, ((3, 0, 0, 18),), 0),
            (3, 3, 19, 0, 8, ((9, 1, 8, 23), (3, 0, 8, 19)), 0),
        ),
        ((0, 0, 3), (1, 1, 3), (4, 0, 7), (5, 0, 15), (12, 0, 13), (13, 0, 5), (14, 0, 11), (15, 1, 2), (16, 1, 5), (17, 1, 4), (20, 0, 9), (21, 0, 1), (22, 1, 0), (23, 1, 6)),
    ),
    (
        (
            (0, 0, -1, 0, 3, ((0, 0, 3, 2), (1, 0, 3, 2), (6, 2, 1, 2), (4, 0, 3, 2), (3, 0, 3, 0)), 0),
            (1, 0, 1, 0, 7, ((6, 2, 2, 9), (4, 0, 7, 8), (3, 0, 7, 4)), 0),
            (1, 0, 2, 0, 15, ((4, 0, 15, 9), (1, 0, 15, 8), (3, 0, 15, 5)), 0),
            (2, 1, 5, 0, 13, ((3, 0, 13, 12),), 0),
            (2, 1, 6, 0, 5, ((9, 1, 5, 17), (0, 0, 5, 14), (3, 0, 5, 13)), 0),
            (2, 1, 7, 0, 11, ((2, 1, 11, 19), (3, 0, 11, 14)), 0),
            (2, 1, 8, 1, 14, ((5, 1, 14, 16),), 0),
            (2, 1, 9, 2, 0, ((1, 1, 14, 17),), 0),
            (3, 0, 13, 2, 1, ((0, 1, 12, 16),), 0),
            (3, 1, 14, 1, 11, ((5, 1, 11, 18),), 0),
            (3, 1, 15, 0, 9, ((3, 0, 9, 20),), 0),
            (3, 1, 16, 1, 12, ((5, 1, 12, 20),), 0),
            (3, 2, 17, 0, 1, ((7, 2, 3, 21), (6, 2, 5, 20), (3, 0, 1, 21)), 0),
            (4, 2, 21, 2, 2, ((0, 1, 15, 22),), 0),
        ),
        ((0, 0, 2), (3, 0, 6), (4, 0, 14), (10, 0, 4), (11, 0, 12), (12, 0, 10), (18, 0, 0), (19, 0, 8), (20, 1, 15), (22, 1, 9), (23, 1, 13), (24, 1, 10), (25, 1, 8)),
    ),
    (
        (
            (0, 0, -1, 0, 4, ((1, 0, 4, 3), (0, 0, 4, 3), (4, 0, 4, 1), (3, 0, 4, 0)), 0),
            (1, 0, 1, 2, 0, ((0, 1, 6, 9),), 0),
            (1, 1, 2, 0, 8, ((4, 0, 8, 13), (7, 2, 0, 9), (1, 0, 8, 11), (3, 0, 8, 4)), 0),
            (1, 1, 3, 0, 6, ((1, 0, 6, 13), (3, 0, 6, 6)), 0),
            (1, 1, 4, 0, 0, ((4, 0, 0, 12), (0, 0, 0, 13), (3, 0, 0, 5)), 0),
            (1, 3, 8, 2, 1, ((2, 1, 1, 12),), 0),
            (1, 3, 9, 2, 2, ((0, 1, 4, 16),), 0),
            (2, 2, 10, 0, 12, ((3, 0, 12, 10),), 0),
            (2, 2, 12, 0, 2, ((0, 0, 2, 20), (3, 0, 2, 11)), 0),
            (2, 2, 14, 0, 10, ((3, 0, 10, 12),), 0),
            (3, 1, 17, 0, 14, ((3, 0, 14, 17),), 0),
            (3, 1, 19, 1, 0, ((2, 2, 1, 19),), 0),
            (4, 2, 21, 2, 3, ((2, 1, 7, 25), (8, 2, 1, 22)), 0),
            (5, 2, 22, 1, 6, ((8, 1, 6, 24),), 0),
        ),
        ((0, 0, 5), (5, 0, 9), (6, 0, 1), (7, 0, 7), (11, 0, 13), (13, 0, 3), (15, 0, 11), (16, 1, 1), (18, 1, 7), (20, 0, 15), (23, 1, 3), (24, 1, 2), (25, 1, 4), (26, 1, 5)),
    ),
    (
        (
            (0, 0, -1, 0, 5, ((4, 0, 5, 1), (1, 0, 5, 1), (0, 0, 5, 4), (3, 0, 5, 0)), 0),
            (1, 0, 1, 0, 9, ((4, 0, 9, 10), (3, 0, 9, 5)), 0),
            (1, 0, 2, 0, 7, ((3, 0, 7, 7),), 0),
            (1, 0, 3, 0, 1, ((7, 2, 0, 9), (4, 0, 1, 11), (3, 0, 1, 6)), 0),
            (2, 0, 7, 0, 13, ((3, 0, 13, 11),), 0),
            (2, 1, 8, 0, 3, ((3, 0, 3, 13),), 0),
            (2, 2, 9, 0, 11, ((3, 0, 11, 15),), 0),
            (3, 1, 13, 1, 9, ((5, 1, 9, 20),), 0),
            (3, 1, 14, 2, 0, ((8, 2, 1, 19), (2, 1, 11, 17)), 0),
            (3, 1, 15, 0, 15, ((3, 0, 15, 20),), 0),
            (3, 2, 16, 1, 8, ((2, 2, 0, 18), (8, 1, 8, 21)), 0),
            (4, 2, 18, 1, 13, ((8, 1, 13, 23),), 0),
            (4, 2, 19, 1, 11, ((5, 1, 11, 23),), 0),
            (4, 2, 20, 1, 10, ((8, 1, 10, 24),), 0),
            (4, 3, 21, 1, 12, ((5, 1, 12, 24),), 0),
            (6, 0, 23, 1, 14, ((5, 1, 14, 25),), 0),
        ),
        ((0, 0, 4), (4, 0, 8), (5, 0, 0), (6, 0, 6), (10, 0, 12), (11, 0, 2), (12, 0, 10), (17, 0, 14), (22, 1, 15)),
    ),
    (
        (
            (0, 0, -1, 0, 6, ((1, 0, 6, 2), (0, 0, 6, 3), (4, 0, 6, 3), (3, 0, 6, 0)), 0),
            (1, 0, 1, 0, 4, ((3, 0, 4, 4),), 0),
            (1, 0, 2, 0, 2, ((3, 0, 2, 5),), 0),
            (1, 1, 3, 0, 10, ((9, 2, 0, 8), (3, 0, 10, 6)), 0),
            (2, 1, 9, 1, 2, ((8, 1, 2, 19), (2, 2, 0, 13)), 0),
            (2, 2, 10, 0, 14, ((3, 0, 14, 12),), 0),
            (2, 2, 12, 0, 0, ((0, 0, 0, 15), (1, 0, 0, 18), (3, 0, 0, 13)), 0),
            (2, 2, 13, 0, 8, ((1, 0, 8, 19), (3, 0, 8, 14)), 0),
            (3, 2, 16, 0, 12, ((3, 0, 12, 18),), 0),
            (5, 3, 20, 2, 0, ((4, 1, 2, 24),), 0),
            (5, 3, 22, 2, 1, ((2, 1, 5, 25), (4, 1, 5, 26)), 0),
        ),
        ((0, 0, 7), (4, 0, 5), (5, 0, 3), (6, 0, 11), (7, 1, 3), (8, 1, 5), (11, 0, 15), (14, 0, 9), (15, 0, 1), (17, 1, 7), (18, 0, 13), (19, 1, 1), (21, 1, 6), (23, 1, 0), (24, 1, 4)),
    ),
    (
        (
            (0, 0, -1, 0, 7, ((7, 2, 0, 1), (1, 0, 7, 1), (0, 0, 7, 4), (4, 0, 7, 2), (3, 0, 7, 0)), 0),
            (1, 0, 1, 0, 5, ((1, 0, 5, 6), (0, 0, 5, 12), (3, 0, 5, 4)), 0),
            (1, 0, 2, 0, 3, ((0, 0, 3, 13), (3, 0, 3, 5)), 0),
            (1, 0, 3, 0, 11, ((1, 0, 11, 7), (3, 0, 11, 6)), 0),
            (2, 0, 7, 1, 11, ((4, 2, 0, 14), (8, 1, 11, 13)), 0),
            (2, 1, 8, 0, 15, ((4, 0, 15, 15), (3, 0, 15, 11)), 0),
            (2, 1, 9, 2, 0, ((5, 2, 0, 13),), 0),
            (2, 1, 10, 0, 9, ((2, 2, 1, 13), (3, 0, 9, 14)), 0),
            (2, 1, 11, 0, 1, ((3, 0, 1, 15),), 0),
            (3, 1, 15, 0, 13, ((3, 0, 13, 18),), 0),
            (3, 1, 16, 1, 9, ((8, 1, 9, 19),), 0),
            (3, 3, 17, 1, 14, ((8, 1, 14, 21),), 0),
            (4, 2, 19, 2, 1, ((2, 1, 9, 19),), 0),
            (4, 2, 20, 1, 13, ((8, 1, 13, 22),), 0),
            (4, 3, 22, 1, 12, ((8, 1, 12, 23),), 0),
        ),
        ((0, 0, 6), (4, 0, 4), (5, 0, 2), (6, 0, 10), (12, 0, 14), (13, 0, 0), (14, 0, 8), (18, 0, 12), (21, 1, 10), (23, 1, 15), (24, 1, 8)),
    ),
    (
        (
            (0, 0, -1, 0, 8, ((0, 0, 8, 2), (4, 0, 8, 2), (1, 0, 8, 2), (3, 0, 8, 0)), 0),
            (1, 0, 1, 0, 12, ((3, 0, 12, 5),), 0),
            (1, 1, 2, 0, 10, ((1, 0, 10, 9), (0, 0, 10, 14), (3, 0, 10, 7)), 0),
            (1, 1, 3, 0, 4, ((4, 0, 4, 9), (3, 0, 4, 6)), 0),
            (2, 0, 7, 2, 0, ((2, 2, 1, 13),), 0),
            (2, 0, 8, 0, 14, ((0, 0, 14, 17), (3, 0, 14, 12)), 0),
            (2, 1, 9, 1, 6, ((8, 1, 6, 13), (5, 1, 6, 15)), 0),
            (2, 1, 10, 1, 7, ((5, 1, 7, 14), (8, 1, 7, 14)), 0),
            (2, 2, 12, 0, 6, ((1, 0, 6, 14), (3, 0, 6, 13)), 0),
            (2, 2, 13, 0, 0, ((3, 0, 0, 14),), 0),
            (3, 2, 17, 2, 1, ((2, 2, 2, 21),), 0),
            (3, 2, 18, 1, 3, ((5, 1, 3, 19),), 0),
            (3, 2, 19, 1, 2, ((5, 1, 2, 20),), 0),
            (3, 3, 20, 0, 2, ((3, 0, 2, 19),), 0),
            (4, 2, 22, 1, 0, ((8, 1, 0, 19), (5, 1, 0, 21)), 0),
            (4, 3, 23, 1, 1, ((8, 1, 1, 20), (5, 1, 1, 22)), 0),
        ),
        ((0, 0, 9), (4, 0, 13), (5, 0, 5), (6, 0, 11), (11, 0, 15), (14, 0, 7), (15, 0, 1), (16, 1, 4), (21, 0, 3), (24, 1, 5)),
    ),
    (
        (
            (0, 0, -1, 0, 9, ((0, 0, 9, 1), (1, 0, 9, 1), (4, 0, 9, 3), (3, 0, 9, 0)), 0),
            (1, 0, 1, 1, 11, ((8, 1, 11, 11),), 0),
            (1, 0, 2, 0, 13, ((4, 0, 13, 10), (0, 0, 13, 7), (3, 0, 13, 4)), 0),
            (1, 0, 3, 0, 11, ((1, 0, 11, 7), (0, 0, 11, 9), (3, 0, 11, 6)), 0),
            (1, 0, 4, 0, 5, ((1, 0, 5, 8), (3, 0, 5, 5)), 0),
            (2, 0, 8, 0, 15, ((3, 0, 15, 11),), 0),
            (2, 0, 9, 2, 0, ((2, 1, 11, 15), (4, 1, 11, 18)), 0),
            (2, 1, 10, 0, 7, ((3, 0, 7, 14),), 0),
            (2, 1, 11, 0, 1, ((3, 0, 1, 15),), 0),
            (3, 2, 17, 1, 12, ((8, 1, 12, 22),), 0),
            (3, 2, 18, 0, 3, ((3, 0, 3, 21),), 0),
            (5, 2, 22, 2, 1, ((2, 1, 15, 23),), 0),
        ),
        ((0, 0, 8), (5, 0, 12), (6, 0, 4), (7, 0, 10), (12, 0, 14), (13, 0, 6), (14, 0, 0), (15, 1, 10), (16, 1, 13), (19, 0, 2), (20, 1, 14), (21, 1, 15), (23, 1, 9), (24, 1, 8)),
    ),
    (
        (
            (0, 0, -1, 0, 10, ((0, 0, 10, 3), (1, 0, 10, 3), (4, 0, 10, 2), (3, 0, 10, 0)), 0),
            (1, 0, 1, 0, 14, ((3, 0, 14, 6),), 0),
            (1, 0, 2, 0, 8, ((1, 0, 8, 8), (3, 0, 8, 7)), 0),
            (1, 0, 3, 0, 6, ((4, 0, 6, 12), (1, 0, 6, 9), (3, 0, 6, 8)), 0),
            (2, 1, 7, 0, 12, ((0, 0, 12, 16), (3, 0, 12, 14)), 0),
            (2, 1, 8, 0, 2, ((3, 0, 2, 15),), 0),
            (2, 2, 9, 0, 4, ((3, 0, 4, 16),), 0),
            (3, 2, 13, 1, 4, ((5, 1, 4, 17),), 0),
            (3, 3, 15, 0, 0, ((3, 0, 0, 21),), 0),
            (4, 2, 17, 1, 7, ((8, 1, 7, 24),), 0),
            (4, 3, 18, 2, 0, ((0, 1, 0, 23),), 0),
            (5, 3, 19, 1, 2, ((5, 1, 2, 23),), 0),
            (6, 0, 20, 1, 3, ((5, 1, 3, 24),), 0),
        ),
        ((0, 0, 11), (4, 0, 15), (5, 0, 9), (6, 0, 7), (10, 0, 13), (11, 0, 5), (12, 0, 3), (14, 1, 5), (16, 0, 1), (21, 1, 6), (22, 1, 0), (23, 1, 1)),
    ),
    (
        (
            (0, 0, -1, 0, 11, ((0, 0, 11, 3), (4, 0, 11, 3), (1, 0, 11, 3), (3, 0, 11, 0)), 0),
            (0, 3, 1, 0, 15, ((4, 0, 15, 8), (3, 0, 15, 4)), 0),
            (1, 0, 2, 2, 0, ((0, 1, 11, 7),), 0),
            (1, 0, 3, 0, 9, ((1, 0, 9, 7), (3, 0, 9, 5)), 0),
            (1, 0, 4, 0, 7, ((1, 0, 7, 9), (4, 0, 7, 10), (3, 0, 7, 6)), 0),
            (1, 0, 5, 2, 1, ((8, 2, 0, 9),), 0),
            (2, 0, 9, 1, 8, ((8, 1, 8, 15),), 0),
            (2, 0, 10, 0, 13, ((0, 0, 13, 15), (3, 0, 13, 10)), 0),
            (2, 0, 11, 1, 9, ((5, 1, 9, 12), (2, 2, 4, 17)), 0),
            (2, 0, 12, 0, 5, ((3, 0, 5, 11),), 0),
            (2, 1, 13, 0, 3, ((4, 0, 3, 18), (3, 0, 3, 12)), 0),
            (3, 1, 17, 1, 12, ((8, 1, 12, 20),), 0),
            (3, 1, 19, 0, 1, ((3, 0, 1, 16),), 0),
            (3, 2, 20, 1, 13, ((5, 1, 13, 19), (8, 1, 13, 21)), 0),
            (4, 2, 22, 1, 14, ((5, 1, 14, 22),), 0),
        ),
        ((0, 0, 10), (6, 0, 14), (7, 0, 8), (8, 0, 6), (14, 0, 12), (15, 0, 2), (16, 0, 4), (18, 1, 11), (21, 0, 0), (23, 1, 10), (24, 1, 15)),
    ),
    (
        (
            (0, 0, -1, 0, 12, ((0, 0, 12, 5), (4, 0, 12, 1), (1, 0, 12, 1), (3, 0, 12, 0)), 0),
            (0, 3, 1, 0, 14, ((0, 0, 14, 10), (1, 0, 14, 8), (3, 0, 14, 3)), 0),
            (1, 0, 2, 0, 8, ((3, 0, 8, 4),), 0),
            (1, 1, 3, 0, 0, ((4, 0, 0, 7), (2, 2, 0, 9), (3, 0, 0, 5)), 0),
            (2, 1, 6, 0, 2, ((3, 0, 2, 9),), 0),
            (2, 1, 7, 0, 4, ((3, 0, 4, 10),), 0),
            (2, 1, 8, 2, 0, ((1, 1, 3, 18),), 0),
            (2, 2, 9, 0, 10, ((3, 0, 10, 11),), 0),
            (3, 1, 13, 2, 1, ((1, 1, 0, 22),), 0),
            (3, 2, 14, 0, 6, ((5, 2, 0, 18), (3, 0, 6, 16)), 0),
            (5, 2, 19, 1, 0, ((5, 1, 0, 21),), 0),
            (5, 3, 20, 1, 1, ((8, 1, 1, 23),), 0),
            (5, 3, 21, 1, 7, ((5, 1, 7, 23),), 0),
            (6, 0, 22, 1, 6, ((5, 1, 6, 22),), 0),
        ),
        ((0, 0, 13), (4, 0, 9), (5, 0, 1), (10, 0, 3), (11, 0, 11), (12, 0, 5), (15, 0, 7), (16, 0, 15), (17, 1, 2), (18, 1, 3), (23, 1, 4), (24, 1, 5)),
    ),
    (
        (
            (0, 0, -1, 0, 13, ((5, 2, 0, 2), (1, 0, 13, 2), (4, 0, 13, 1), (0, 0, 13, 3), (3, 0, 13, 0)), 0),
            (0, 3, 1, 0, 9, ((0, 0, 9, 7), (3, 0, 9, 4)), 0),
            (1, 0, 2, 0, 1, ((4, 0, 1, 8), (1, 0, 1, 11), (3, 0, 1, 5)), 0),
            (2, 1, 6, 0, 3, ((3, 0, 3, 10),), 0),
            (2, 1, 7, 0, 11, ((0, 0, 11, 15), (3, 0, 11, 11)), 0),
            (2, 1, 8, 0, 5, ((3, 0, 5, 12),), 0),
            (3, 0, 12, 1, 15, ((4, 2, 0, 18), (8, 1, 15, 17)), 0),
            (3, 1, 13, 2, 0, ((4, 1, 11, 20),), 0),
            (3, 1, 14, 0, 7, ((3, 0, 7, 15),), 0),
            (3, 1, 15, 0, 15, ((3, 0, 15, 16),), 0),
            (4, 1, 18, 2, 1, ((8, 2, 2, 21), (2, 1, 8, 19)), 0),
            (4, 2, 19, 1, 11, ((2, 2, 0, 20), (8, 1, 11, 23)), 0),
            (4, 2, 20, 2, 2, ((8, 2, 3, 24), (2, 1, 15, 21)), 0),
            (5, 3, 22, 1, 8, ((8, 1, 8, 26),), 0),
            (5, 3, 23, 1, 9, ((5, 1, 9, 24),), 0),
        ),
        ((0, 0, 12), (3, 0, 14), (4, 0, 8), (5, 0, 0), (9, 0, 2), (10, 0, 4), (11, 0, 10), (16, 0, 6), (17, 1, 10), (21, 1, 14), (24, 1, 13), (25, 1, 12)),
    ),
    (
        (
            (0, 0, -1, 0, 14, ((4, 0, 14, 1), (0, 0, 14, 3), (1, 0, 14, 1), (3, 0, 14, 0)), 0),
            (1, 0, 1, 0, 12, ((0, 0, 12, 10), (1, 0, 12, 7), (3, 0, 12, 4)), 0),
            (1, 0, 2, 0, 2, ((1, 0, 2, 8), (4, 0, 2, 6), (3, 0, 2, 5)), 0),
            (1, 0, 3, 0, 10, ((0, 0, 10, 11), (3, 0, 10, 6)), 0),
            (2, 1, 7, 0, 0, ((5, 2, 1, 17), (3, 0, 0, 10)), 0),
            (2, 2, 8, 0, 8, ((3, 0, 8, 11),), 0),
            (2, 2, 9, 0, 6, ((3, 0, 6, 13),), 0),
            (3, 1, 13, 0, 4, ((3, 0, 4, 15),), 0),
            (3, 2, 14, 1, 1, ((8, 1, 1, 18),), 0),
            (4, 2, 18, 2, 0, ((4, 1, 1, 20),), 0),
            (4, 3, 19, 1, 5, ((8, 1, 5, 21),), 0),
            (4, 3, 20, 1, 4, ((8, 1, 4, 22),), 0),
        ),
        ((0, 0, 15), (4, 0, 13), (5, 0, 3), (6, 0, 11), (10, 0, 9), (11, 0, 1), (12, 0, 7), (15, 1, 0), (16, 0, 5), (17, 1, 2), (21, 1, 6), (22, 1, 7), (23, 1, 3)),
    ),
    (
        (
            (0, 0, -1, 0, 15, ((0, 0, 15, 2), (2, 2, 0, 1), (1, 0, 15, 1), (3, 0, 15, 0)), 0),
            (0, 3, 1, 0, 13, ((2, 2, 2, 9), (3, 0, 13, 4)), 0),
            (0, 3, 2, 0, 3, ((7, 2, 0, 7), (3, 0, 3, 5)), 0),
            (1, 0, 3, 0, 11, ((3, 0, 11, 6),), 0),
            (2, 0, 7, 0, 9, ((0, 0, 9, 15), (3, 0, 9, 10)), 0),
            (2, 0, 8, 0, 1, ((0, 0, 1, 17), (1, 0, 1, 19), (3, 0, 1, 11)), 0),
            (2, 1, 9, 0, 7, ((4, 0, 7, 14), (3, 0, 7, 12)), 0),
            (3, 0, 12, 1, 8, ((4, 2, 1, 18), (8, 1, 8, 17)), 0),
            (3, 1, 14, 0, 5, ((3, 0, 5, 16),), 0),
            (4, 1, 16, 1, 12, ((8, 1, 12, 21),), 0),
            (4, 1, 18, 2, 0, ((2, 1, 15, 22),), 0),
            (4, 2, 19, 2, 1, ((5, 2, 1, 22), (4, 1, 9, 23)), 0),
            (5, 1, 21, 2, 2, ((2, 1, 10, 23),), 0),
            (5, 3, 22, 1, 15, ((5, 1, 15, 23), (8, 1, 15, 24)), 0),
            (5, 3, 24, 2, 3, ((2, 1, 13, 25),), 0),
            (5, 3, 25, 1, 14, ((5, 1, 14, 24),), 0),
        ),
        ((0, 0, 14), (4, 0, 12), (5, 0, 2), (6, 0, 10), (10, 0, 0), (11, 0, 8), (13, 0, 6), (15, 0, 4), (17, 1, 13), (20, 1, 11), (23, 1, 9), (26, 1, 10)),
    ),
)
VMEM_LIMIT = 24 << 20
MBV, NBV = 256, 1024

F32, BF16 = jnp.float32, jnp.bfloat16
MESH = pl.DeviceIdType.MESH
NT_PTS = 3
PAIRS, ROWS, COLS, OWN = 2048, 2048, 1024, 128
KC = PAIRS // NC
KK = 512
NK = PAIRS // KK
PER = KK // KC
MB, NB = MBV, NBV
NM = ROWS // MB
START = SMAX + PER
STEPS = NC + SMAX


def flip(value, bits):
    return [jnp.int32(b) * (1 - 2 * ((value // b) % 2)) for b in bits]


def flipped(value, deltas, bits, mask):
    for delta, bit in zip(deltas, bits):
        if mask & bit:
            value = value + delta
    return value


def weigh(x, factor, w_ref):
    x = x.astype(F32)
    for t in range(NT_PTS):
        w_ref[pl.ds(t * MB, MB), :] = (x * factor(t)).astype(BF16)


def product(w, y):
    return lax.dot_general(w, y, (((1,), (1,)), ((), ())), preferred_element_type=F32)


def gather_kernel(points, weights, own_ref, den_ref, acc, x_ref, y_ref, f_ref,
                  transit, w_ref, send_sem, recv_sem, local_sem):
    row, col = lax.axis_index("row"), lax.axis_index("col")
    row_d, col_d = flip(row, (1, 2, 4)), flip(col, (1, 2, 4, 8))
    peers = [
        {"row": flipped(row, row_d, (1, 2, 4), dr), "col": flipped(col, col_d, (1, 2, 4, 8), dc)}
        for dr, dc in TARGETS
    ]
    barrier = pltpu.get_barrier_semaphore()
    for peer in peers:
        pl.semaphore_signal(barrier, inc=1, device_id=peer, device_id_type=MESH)

    high = row // 4
    code = row * 2 + high
    code_d = flip(code, (1, 2, 4, 8))

    def lanes(j):
        return pl.ds(pl.multiple_of((j % PER) * KC, KC), KC)

    def place(kind, mark, j):
        if kind == 2:
            return transit.at[j, mark]
        slot = flipped(code, code_d, (1, 2, 4, 8), mark)
        if kind == 0:
            return x_ref.at[j // PER, pl.ds(pl.multiple_of(slot * OWN, OWN), OWN), lanes(j)]
        slot = slot % 8
        return y_ref.at[j // PER, pl.ds(pl.multiple_of(slot * OWN, OWN), OWN), lanes(j)]

    for k in range(NK):
        x_ref[k, pl.ds(pl.multiple_of(col * OWN, OWN), OWN), :] = own_ref[pl.ds(k * KK, KK), :].T
    for t in range(NT_PTS):
        f_ref[t] = weights[t] * jnp.exp(-points[t] * den_ref[...])
    pl.semaphore_wait(barrier, len(TARGETS))

    k_col = col // 2
    bits = [((row // b) % 2 + (k_col // b) % 2) % 2 for b in (4, 2, 1)]
    which = (bits[0] * 4 + bits[1] * 2 + bits[2]) * 2 + ((col % 2) + high) % 2

    def arrived(kind, mark, event, j):
        ref = place(kind, mark, j)
        pltpu.make_async_copy(ref, ref, recv_sem.at[j, event]).wait()

    def act(action, j):
        _, _, event, kind, mark, kids, local = action
        if event >= 0:
            arrived(kind, mark, event, j)
        src = place(kind, mark, j)
        for target, to_kind, to_mark, to_event in kids:
            pltpu.make_async_remote_copy(
                src_ref=src, dst_ref=place(to_kind, to_mark, j),
                send_sem=send_sem.at[j], recv_sem=recv_sem.at[j, to_event],
                device_id=peers[target], device_id_type=MESH,
            ).start()
        if local:
            pltpu.make_async_copy(src, place(1, mark, j), local_sem.at[j]).start()

    def bulk_wait(sem, copies):
        ref = acc.at[0, pl.ds(0, copies * OWN * KC // (2 * COLS)), :]
        pltpu.make_async_copy(ref, ref, sem).wait()

    def settle(j):
        for g, (actions, last) in enumerate(PROGRAMS):
            @pl.when(which == g)
            def _():
                for event, kind, mark in last:
                    arrived(kind, mark, event, j)
                copies = sum(a[6] for a in actions)
                if copies:
                    bulk_wait(local_sem.at[j], copies)

    def block(k, m):
        rows = pl.ds(pl.multiple_of(m * MB, MB), MB)
        weigh(x_ref[k, rows, :], lambda t: f_ref[t, pl.ds(k, 1), :], w_ref)

        @pl.loop(0, COLS // NB)
        def _(n):
            at = pl.ds(pl.multiple_of(n * NB, NB), NB)
            for t in range(NT_PTS):
                acc[t, rows, at] += product(w_ref[pl.ds(t * MB, MB), :], y_ref[k, at, :])

    @pl.loop(0, STEPS)
    def _(p):
        k = jnp.maximum(p - START, 0) // PER
        part = jnp.maximum(p - START, 0) % PER
        busy = p >= START

        @pl.when(jnp.logical_and(busy, part == 0))
        def _():
            for i in range(PER):
                settle(k * PER + i)

        @pl.loop(0, NG)
        def _(group):
            for g, (actions, _last) in enumerate(PROGRAMS):
                @pl.when(which == g)
                def _():
                    for at in range(NG):
                        mine = [a for a in actions if a[1] == at]
                        for lag in sorted({a[0] for a in mine}):
                            @pl.when(jnp.logical_and(group == at, jnp.logical_and(p >= lag, p < NC + lag)))
                            def _():
                                for a in mine:
                                    if a[0] == lag:
                                        act(a, p - lag)

            @pl.when(jnp.logical_and(p == 0, group == 0))
            def _():
                @pl.loop(0, ROWS // 64)
                def _(m):
                    at = pl.ds(pl.multiple_of(m * 64, 64), 64)
                    acc[:, at, :] = jnp.zeros((NT_PTS, 64, COLS), F32)

            @pl.when(busy)
            def _():
                for b in range(NM // PER // NG):
                    block(k, (part * NG + group) * (NM // PER // NG) + b)

    for i in range(PER):
        settle(NC - PER + i)
    for g, (actions, _last) in enumerate(PROGRAMS):
        @pl.when(which == g)
        def _():
            @pl.loop(0, NC)
            def _(j):
                bulk_wait(send_sem.at[j], sum(len(a[5]) for a in actions))


def last_kernel(acc, x_ref, y_ref, f_ref, out, w_ref, buf, sem):
    def copy(m, slot):
        return pltpu.make_async_copy(
            buf.at[slot], out.at[:, pl.ds(pl.multiple_of(m * MB, MB), MB), :], sem.at[slot]
        )

    @pl.loop(0, NM)
    def _(m):
        slot = m % 2
        rows = pl.ds(pl.multiple_of(m * MB, MB), MB)
        weigh(x_ref[NK - 1, rows, :], lambda t: f_ref[t, NK - 1:NK, :], w_ref)

        @pl.when(m >= 2)
        def _():
            copy(m - 2, slot).wait()

        @pl.loop(0, COLS // NB)
        def _(n):
            at = pl.ds(pl.multiple_of(n * NB, NB), NB)
            for t in range(NT_PTS):
                d = product(w_ref[pl.ds(t * MB, MB), :], y_ref[NK - 1, at, :])
                buf[slot, t, :, at] = acc[t, rows, at] + d

        copy(m, slot).start()

    copy(NM - 2, 0).wait()
    copy(NM - 1, 1).wait()


def on_device(pair_ints, denominators, lap_points, lap_weights):
    vmem = pl.BlockSpec(memory_space=pltpu.VMEM)
    smem = pl.BlockSpec(memory_space=pltpu.SMEM)
    held = pl.pallas_call(
        gather_kernel,
        out_shape=(
            pltpu.VMEM((NT_PTS, ROWS, COLS), F32),
            pltpu.VMEM((NK, ROWS, KK), BF16),
            pltpu.VMEM((NK, COLS, KK), BF16),
            pltpu.VMEM((NT_PTS, NK, KK), F32),
        ),
        in_specs=[smem, smem, vmem, vmem],
        out_specs=(vmem,) * 4,
        scratch_shapes=[
            pltpu.VMEM((NC, NT, OWN, KC), BF16),
            pltpu.VMEM((NT_PTS * MB, KK), BF16),
            pltpu.SemaphoreType.DMA((NC,)),
            pltpu.SemaphoreType.DMA((NC, NE)),
            pltpu.SemaphoreType.DMA((NC,)),
        ],
        compiler_params=pltpu.CompilerParams(
            collective_id=0, has_side_effects=True, vmem_limit_bytes=VMEM_LIMIT
        ),
    )(lap_points, lap_weights, pair_ints, denominators.reshape(NK, KK))
    held = [pltpu.with_memory_space_constraint(a, pltpu.VMEM) for a in held]
    return pl.pallas_call(
        last_kernel,
        out_shape=jax.ShapeDtypeStruct((NT_PTS, ROWS, COLS), F32),
        in_specs=[vmem] * 4,
        out_specs=pl.BlockSpec(memory_space=pl.ANY),
        scratch_shapes=[
            pltpu.VMEM((NT_PTS * MB, KK), BF16),
            pltpu.VMEM((2, NT_PTS, MB, COLS), F32),
            pltpu.SemaphoreType.DMA((2,)),
        ],
        compiler_params=pltpu.CompilerParams(vmem_limit_bytes=VMEM_LIMIT),
    )(*held)


def solution(mesh):
    in_specs = (P(None, ("row", "col")), P(), P(), P())
    out_specs = P(None, "row", "col")
    return jax.shard_map(
        on_device, mesh=mesh, in_specs=in_specs, out_specs=out_specs, check_vma=False
    )
```

time: 197 us -> 94.6 us (0.48); the launches traced: 194 us -> 94.5 us
  Pallas kernels: 0 us -> 93.2 us
  waiting for transfers between devices: 89.6 us -> 0 us
  blocking collectives: 42 us -> 0 us
  matrix products: 33.6 us -> 0 us
  between operations: 13.4 us -> 0.01 us
  local copies, waits for them, and re-layouts: 13.7 us -> 1.3 us
    pallas_call x0 -> x2, Pallas kernels: none -> 93.2 us  [the longest x1 81.2 us: on_device(): pl.pallas_call(gather_kernel, out_shape=(pltpu.VMEM((NT_PTS, ROWS, COLS),...]
    all_gather x2 -> x0, waiting for transfers between devices: 88.9 us -> none  [the longest x1 58.4 us: on_device(): col_whole = lax.all_gather(col_block, 'row', axis=0, tiled=True)]
    all_to_all x2 -> x0, blocking collectives: 42 us -> none  [the longest x1 23 us: on_device(): lax.all_to_all(pair_ints, ('row', 'col'), split_axis=0, concat_axis=1, ti...]
    dot_general x1 -> x0, matrix products: 33.6 us -> none  [on_device(): jnp.einsum('trp,rq->tpq', weighted, col_whole, preferred_element_type=jnp...]
    convert_element_type x1 -> x0, local copies, waits for them, and re-layouts: 13 us -> none  [on_device(): lax.all_gather(pair_ints, 'col', axis=1, tiled=True).astype(jnp.float32)]
  transfers between devices with their start and end apart: 2 -> 0, of which waited for: 2 -> 0; matrix products, arithmetic and copies ran while one was open for 8% -> 0% of each run, Pallas kernels for 0% -> 0%
where the time goes in v2:
time: 94.6 us; the launch traced here: 94.5 us
  Pallas kernels  93.2 us (99%)
  local copies, waits for them, and re-layouts  1.3 us (1%)
    pallas_call x1, Pallas kernels, on_device(): pl.pallas_call(gather_kernel, out_shape=(pltpu.VMEM((NT_PTS, ROWS, COLS),...  81.2 us
    pallas_call x1, Pallas kernels, on_device(): pl.pallas_call(last_kernel, out_shape=jax.ShapeDtypeStruct((NT_PTS, ROWS,...  12 us

profile of v2, /device:TPU:36, one launch (start us, length us, event | category | flops | bytes accessed | tf_op | source)
XLA Modules:
  0.0 94.5 jit_solution(10077376632437322208)
XLA Ops:
  0.0 1.3 %reshape.3.den_ref = f32[4,512]{1,0:T(4,128)} reshape(f32[2048]{0:T(1024)} %param.5) | data formatting | bytes 16384 | tf_op jit(solution)/shard_map/reshape | solution.py:535
  1.3 81.2 %shard_map.46 = (f32[3,2048,1024]{2,1,0:T(8,128)S(1)}, bf16[4,2048,512]{2,1,0:T(8,128)(2,1)S(1)}, bf16[4,1024,512]{2,1,0:T(8,128)(2,1)S(1)}, f32[3,4,512]{2,1,0:T(4,128)S(1)}) custom-call(f32[3]{0:T(128)} %points.1, f32[3]{0:T(128)} %weights.1, bf16[2048,128]{1,0:T(8,128)(2,1)} %own_ref.1, f32[4,512]{1,0:T(4,128)} %reshape.3.den_ref), custom_call_target="tpu_custom_call" | custom-call | tf_op jit(solution)/shard_map/pallas_call | solution.py:515
  82.5 12.0 %shard_map.47 = f32[3,2048,1024]{2,1,0:T(8,128)} custom-call(f32[3,2048,1024]{2,1,0:T(8,128)S(1)} %get-tuple-element.9.acc, bf16[4,2048,512]{2,1,0:T(8,128)(2,1)S(1)} %get-tuple-element.10.x_ref, bf16[4,1024,512]{2,1,0:T(8,128)(2,1)S(1)} %get-tuple-element.11.y_ref, f32[3,4,512]{2,1,0:T(4,128)S(1)} %get-tuple-element.12.f_ref), custom_call_target="tpu_custom_call" | custom-call | tf_op jit(solution)/shard_map/pallas_call | solution.py:537

commit v3 on v0

v3 whole, which is shorter than its diff:
```python
import itertools

import jax
import jax.numpy as jnp
from jax import lax
from jax.experimental import pallas as pl
from jax.experimental.pallas import tpu as pltpu
from jax.sharding import PartitionSpec as P

NC, NG, SMAX, NT, NE = 8, 2, 8, 6, 27
TARGETS = ((0, 12), (0, 4), (4, 2), (0, 1), (3, 0), (0, 2), (1, 1), (3, 1), (1, 0), (4, 3))
PROGRAMS = (
    (
        (
            (0, 0, -1, 0, 0, ((0, 0, 0, 2), (1, 0, 0, 5), (2, 2, 1, 5), (3, 0, 0, 0)), 1),
            (1, 0, 1, 2, 0, ((1, 2, 1, 8),), 0),
            (4, 0, 18, 0, 10, ((7, 1, 10, 22), (3, 0, 10, 16)), 0),
            (3, 0, 15, 0, 7, (), 1),
            (1, 0, 2, 0, 4, ((4, 1, 4, 8), (5, 0, 4, 7), (0, 0, 4, 6), (3, 0, 4, 4)), 1),
            (1, 0, 3, 2, 1, ((2, 1, 1, 10), (5, 1, 1, 9)), 0),
            (2, 0, 9, 0, 14, ((6, 1, 14, 15), (3, 0, 14, 10)), 0),
            (1, 0, 4, 0, 2, ((1, 0, 2, 11), (3, 0, 2, 6)), 1),
            (2, 0, 10, 2, 2, ((2, 1, 5, 18), (5, 1, 5, 16)), 0),
            (1, 0, 5, 0, 12, ((6, 1, 12, 6), (1, 0, 12, 10), (3, 0, 12, 5)), 0),
            (0, 0, 0, 0, 1, (), 1),
            (2, 0, 11, 0, 6, ((3, 0, 6, 11),), 1),
            (1, 0, 6, 0, 5, (), 1),
            (2, 1, 12, 0, 8, ((3, 0, 8, 12),), 0),
            (3, 1, 17, 2, 4, ((5, 1, 0, 22),), 0),
            (2, 1, 13, 2, 3, ((2, 1, 4, 20), (5, 1, 4, 17)), 0),
            (1, 1, 8, 0, 3, (), 1),
            (4, 1, 20, 2, 5, ((2, 1, 3, 23),), 0),
        ),
        ((7, 0, 13), (14, 0, 15), (16, 0, 9), (19, 0, 11)),
    ),
    (
        (
            (0, 0, -1, 0, 1, ((0, 0, 1, 1), (1, 0, 1, 3), (6, 1, 1, 2), (3, 0, 1, 0)), 0),
            (1, 0, 1, 0, 5, ((6, 1, 5, 6), (7, 1, 5, 7), (3, 0, 5, 6)), 0),
            (3, 0, 12, 0, 8, (), 1),
            (1, 0, 2, 0, 3, ((1, 0, 3, 8), (0, 0, 3, 7), (7, 1, 3, 9), (3, 0, 3, 8)), 0),
            (1, 0, 3, 0, 13, ((5, 0, 13, 5), (3, 0, 13, 7)), 1),
            (2, 0, 7, 0, 15, ((4, 1, 15, 15), (0, 0, 15, 13), (3, 0, 15, 14)), 1),
            (4, 1, 16, 0, 10, (), 1),
            (2, 1, 8, 0, 7, ((3, 0, 7, 15),), 0),
            (2, 1, 9, 0, 9, ((8, 1, 9, 16), (3, 0, 9, 16)), 1),
            (3, 1, 13, 2, 0, ((0, 2, 2, 19),), 0),
            (3, 1, 14, 2, 1, ((2, 1, 14, 17),), 0),
            (2, 1, 10, 0, 14, (), 1),
            (1, 1, 5, 0, 12, (), 1),
            (3, 1, 15, 0, 11, ((4, 1, 11, 20), (8, 1, 11, 22), (3, 0, 11, 19)), 1),
        ),
        ((0, 0, 0), (4, 0, 4), (6, 0, 2), (11, 0, 6)),
    ),
    (
        (
            (0, 0, -1, 0, 2, ((2, 1, 2, 1), (5, 0, 2, 4), (0, 0, 2, 1), (1, 0, 2, 1), (3, 0, 2, 0)), 0),
            (2, 0, 6, 1, 7, ((4, 1, 7, 16),), 0),
            (1, 0, 1, 0, 14, ((9, 1, 14, 10), (1, 0, 14, 10), (3, 0, 14, 3)), 0),
            (1, 0, 3, 0, 6, ((8, 2, 3, 13), (3, 0, 6, 4)), 0),
            (4, 0, 20, 0, 8, ((9, 1, 8, 23), (3, 0, 8, 18)), 0),
            (4, 0, 21, 0, 0, ((3, 0, 0, 19),), 0),
            (2, 0, 7, 0, 4, ((0, 0, 4, 13), (2, 1, 4, 16), (3, 0, 4, 10)), 0),
            (2, 1, 8, 0, 12, ((6, 2, 1, 14), (3, 0, 12, 11)), 0),
            (2, 1, 9, 1, 1, ((4, 1, 1, 19),), 0),
            (2, 1, 10, 2, 0, ((1, 1, 7, 17),), 0),
            (2, 1, 11, 0, 10, ((5, 0, 10, 18), (3, 0, 10, 12)), 0),
        ),
        ((0, 0, 3), (2, 1, 3), (4, 0, 15), (5, 0, 7), (12, 0, 13), (13, 0, 11), (14, 0, 5), (15, 1, 2), (16, 1, 5), (17, 1, 4), (18, 0, 1), (19, 0, 9), (22, 1, 0), (23, 1, 6)),
    ),
    (
        (
            (0, 0, -1, 0, 3, ((0, 0, 3, 1), (1, 0, 3, 1), (6, 2, 1, 3), (5, 0, 3, 2), (3, 0, 3, 0)), 0),
            (1, 0, 1, 0, 15, ((5, 0, 15, 7), (1, 0, 15, 8), (3, 0, 15, 4)), 0),
            (1, 0, 2, 0, 7, ((6, 2, 2, 10), (5, 0, 7, 8), (3, 0, 7, 5)), 0),
            (5, 0, 21, 2, 2, ((0, 1, 15, 24),), 0),
            (2, 1, 5, 0, 13, ((3, 0, 13, 12),), 0),
            (3, 1, 13, 0, 1, ((7, 2, 3, 21), (6, 2, 5, 20), (3, 0, 1, 18)), 0),
            (3, 1, 14, 2, 1, ((0, 1, 12, 16),), 0),
            (2, 1, 6, 1, 14, ((4, 1, 14, 16),), 0),
            (2, 1, 7, 2, 0, ((1, 1, 14, 17),), 0),
            (2, 1, 8, 0, 11, ((2, 1, 11, 18), (3, 0, 11, 13)), 0),
            (3, 1, 15, 1, 12, ((4, 1, 12, 19),), 0),
            (2, 1, 9, 0, 5, ((9, 1, 5, 18), (0, 0, 5, 14), (3, 0, 5, 14)), 0),
            (3, 1, 16, 1, 11, ((4, 1, 11, 20),), 0),
            (3, 1, 17, 0, 9, ((3, 0, 9, 19),), 0),
        ),
        ((0, 0, 2), (3, 0, 14), (4, 0, 6), (10, 0, 4), (11, 0, 12), (12, 0, 10), (18, 0, 8), (19, 0, 0), (20, 1, 15), (22, 1, 9), (23, 1, 13), (24, 1, 10), (25, 1, 8)),
    ),
    (
        (
            (0, 0, -1, 0, 4, ((1, 0, 4, 2), (0, 0, 4, 1), (5, 0, 4, 3), (3, 0, 4, 0)), 0),
            (3, 0, 11, 0, 2, ((0, 0, 2, 20), (3, 0, 2, 11)), 0),
            (3, 0, 12, 0, 10, ((3, 0, 10, 12),), 0),
            (5, 0, 21, 2, 3, ((2, 1, 7, 22), (8, 2, 0, 21)), 0),
            (1, 0, 1, 0, 6, ((1, 0, 6, 11), (3, 0, 6, 4)), 0),
            (1, 0, 2, 2, 0, ((0, 1, 6, 8),), 0),
            (2, 0, 8, 2, 1, ((2, 1, 1, 13),), 0),
            (6, 0, 22, 1, 6, ((8, 1, 6, 24),), 0),
            (1, 0, 3, 0, 8, ((5, 0, 8, 12), (7, 2, 0, 7), (1, 0, 8, 12), (3, 0, 8, 5)), 0),
            (2, 1, 9, 2, 2, ((0, 1, 4, 16),), 0),
            (1, 1, 5, 0, 0, ((5, 0, 0, 13), (0, 0, 0, 13), (3, 0, 0, 6)), 0),
            (3, 1, 17, 0, 14, ((3, 0, 14, 17),), 0),
            (3, 1, 18, 1, 0, ((2, 2, 1, 20),), 0),
            (2, 1, 10, 0, 12, ((3, 0, 12, 10),), 0),
        ),
        ((0, 0, 5), (4, 0, 7), (6, 0, 9), (7, 0, 1), (13, 0, 13), (14, 0, 3), (15, 0, 11), (16, 1, 1), (19, 1, 7), (20, 0, 15), (23, 1, 3), (24, 1, 5), (25, 1, 4), (26, 1, 2)),
    ),
    (
        (
            (0, 0, -1, 0, 5, ((5, 0, 5, 3), (1, 0, 5, 1), (0, 0, 5, 2), (3, 0, 5, 0)), 0),
            (1, 0, 1, 0, 7, ((3, 0, 7, 4),), 0),
            (4, 0, 16, 1, 8, ((2, 2, 0, 18), (8, 1, 8, 21)), 0),
            (5, 0, 18, 1, 11, ((4, 1, 11, 23),), 0),
            (5, 0, 19, 1, 10, ((8, 1, 10, 23),), 0),
            (1, 0, 2, 0, 9, ((5, 0, 9, 10), (3, 0, 9, 6)), 0),
            (5, 0, 20, 1, 13, ((8, 1, 13, 24),), 0),
            (1, 0, 3, 0, 1, ((7, 2, 0, 10), (5, 0, 1, 11), (3, 0, 1, 7)), 0),
            (5, 1, 21, 1, 12, ((4, 1, 12, 24),), 0),
            (2, 1, 7, 0, 13, ((3, 0, 13, 13),), 0),
            (3, 1, 13, 2, 0, ((8, 2, 1, 19), (2, 1, 11, 17)), 0),
            (3, 1, 14, 1, 9, ((4, 1, 9, 20),), 0),
            (2, 1, 8, 0, 3, ((3, 0, 3, 14),), 0),
            (6, 1, 23, 1, 14, ((4, 1, 14, 25),), 0),
            (2, 1, 9, 0, 11, ((3, 0, 11, 15),), 0),
            (3, 1, 15, 0, 15, ((3, 0, 15, 20),), 0),
        ),
        ((0, 0, 4), (4, 0, 6), (5, 0, 8), (6, 0, 0), (10, 0, 12), (11, 0, 2), (12, 0, 10), (17, 0, 14), (22, 1, 15)),
    ),
    (
        (
            (0, 0, -1, 0, 6, ((1, 0, 6, 3), (0, 0, 6, 2), (5, 0, 6, 1), (3, 0, 6, 0)), 0),
            (4, 0, 16, 0, 12, ((3, 0, 12, 18),), 0),
            (3, 0, 12, 0, 8, ((1, 0, 8, 20), (3, 0, 8, 13)), 0),
            (3, 0, 13, 0, 0, ((0, 0, 0, 16), (1, 0, 0, 21), (3, 0, 0, 14)), 0),
            (6, 0, 21, 2, 0, ((2, 1, 5, 24), (5, 1, 5, 24)), 0),
            (1, 0, 1, 0, 2, ((3, 0, 2, 4),), 0),
            (6, 1, 22, 2, 1, ((5, 1, 2, 26),), 0),
            (1, 1, 2, 0, 10, ((9, 2, 0, 8), (3, 0, 10, 5)), 0),
            (1, 1, 3, 0, 4, ((3, 0, 4, 6),), 0),
            (2, 1, 8, 1, 2, ((8, 1, 2, 18), (2, 2, 0, 15)), 0),
            (2, 1, 10, 0, 14, ((3, 0, 14, 12),), 0),
        ),
        ((0, 0, 7), (4, 0, 3), (5, 0, 11), (6, 0, 5), (7, 1, 3), (9, 1, 5), (11, 0, 15), (14, 0, 9), (15, 0, 1), (17, 1, 7), (18, 0, 13), (19, 1, 1), (20, 1, 6), (23, 1, 0), (24, 1, 4)),
    ),
    (
        (
            (0, 0, -1, 0, 7, ((7, 2, 0, 1), (1, 0, 7, 2), (0, 0, 7, 3), (5, 0, 7, 1), (3, 0, 7, 0)), 0),
            (4, 0, 16, 0, 13, ((3, 0, 13, 18),), 0),
            (4, 0, 17, 1, 14, ((8, 1, 14, 21),), 0),
            (1, 0, 1, 0, 3, ((0, 0, 3, 11), (3, 0, 3, 4)), 0),
            (5, 0, 20, 1, 13, ((8, 1, 13, 22),), 0),
            (1, 0, 2, 0, 11, ((1, 0, 11, 8), (3, 0, 11, 5)), 0),
            (2, 0, 7, 1, 11, ((5, 2, 0, 13), (8, 1, 11, 14)), 0),
            (1, 0, 3, 0, 5, ((1, 0, 5, 9), (0, 0, 5, 13), (3, 0, 5, 6)), 0),
            (5, 0, 22, 1, 12, ((8, 1, 12, 23),), 0),
            (2, 1, 8, 0, 15, ((5, 0, 15, 15), (3, 0, 15, 11)), 0),
            (2, 1, 9, 2, 0, ((4, 2, 0, 13),), 0),
            (2, 1, 10, 0, 9, ((2, 2, 1, 14), (3, 0, 9, 14)), 0),
            (2, 1, 11, 0, 1, ((3, 0, 1, 15),), 0),
            (3, 1, 15, 1, 9, ((8, 1, 9, 18),), 0),
            (4, 1, 19, 2, 1, ((2, 1, 9, 19),), 0),
        ),
        ((0, 0, 6), (4, 0, 2), (5, 0, 10), (6, 0, 4), (12, 0, 14), (13, 0, 8), (14, 0, 0), (18, 0, 12), (21, 1, 10), (23, 1, 8), (24, 1, 15)),
    ),
    (
        (
            (0, 0, -1, 0, 8, ((0, 0, 8, 3), (5, 0, 8, 3), (1, 0, 8, 3), (3, 0, 8, 0)), 0),
            (4, 0, 17, 2, 1, ((2, 2, 2, 21),), 0),
            (4, 0, 18, 1, 2, ((4, 1, 2, 19),), 0),
            (4, 0, 19, 1, 3, ((4, 1, 3, 20),), 0),
            (4, 0, 20, 0, 2, ((3, 0, 2, 19),), 0),
            (2, 0, 7, 2, 0, ((2, 2, 1, 14),), 0),
            (1, 0, 1, 0, 4, ((5, 0, 4, 9), (3, 0, 4, 5)), 0),
            (5, 0, 22, 1, 0, ((8, 1, 0, 19), (4, 1, 0, 21)), 0),
            (1, 1, 2, 0, 12, ((3, 0, 12, 6),), 0),
            (2, 1, 8, 1, 6, ((8, 1, 6, 14), (4, 1, 6, 15)), 0),
            (2, 1, 9, 0, 14, ((0, 0, 14, 17), (3, 0, 14, 12)), 0),
            (1, 1, 3, 0, 10, ((1, 0, 10, 9), (0, 0, 10, 12), (3, 0, 10, 7)), 0),
            (2, 1, 10, 1, 7, ((4, 1, 7, 14), (8, 1, 7, 13)), 0),
            (5, 1, 23, 1, 1, ((8, 1, 1, 20), (4, 1, 1, 22)), 0),
            (2, 1, 12, 0, 6, ((1, 0, 6, 13), (3, 0, 6, 13)), 0),
            (2, 1, 13, 0, 0, ((3, 0, 0, 14),), 0),
        ),
        ((0, 0, 9), (4, 0, 5), (5, 0, 13), (6, 0, 11), (11, 0, 15), (14, 0, 1), (15, 0, 7), (16, 1, 4), (21, 0, 3), (24, 1, 5)),
    ),
    (
        (
            (0, 0, -1, 0, 9, ((0, 0, 9, 2), (1, 0, 9, 2), (5, 0, 9, 4), (3, 0, 9, 0)), 0),
            (4, 0, 18, 1, 12, ((8, 1, 12, 22),), 0),
            (1, 0, 1, 1, 11, ((8, 1, 11, 9),), 0),
            (1, 0, 2, 0, 5, ((1, 0, 5, 6), (3, 0, 5, 4)), 0),
            (2, 0, 8, 0, 15, ((3, 0, 15, 11),), 0),
            (1, 0, 3, 0, 13, ((5, 0, 13, 12), (0, 0, 13, 7), (3, 0, 13, 5)), 0),
            (1, 0, 4, 0, 11, ((1, 0, 11, 8), (0, 0, 11, 9), (3, 0, 11, 6)), 0),
            (2, 0, 9, 2, 0, ((2, 1, 11, 15), (5, 1, 11, 19)), 0),
            (2, 0, 10, 0, 1, ((3, 0, 1, 14),), 0),
            (6, 0, 22, 2, 1, ((2, 1, 15, 23),), 0),
            (2, 0, 11, 0, 7, ((3, 0, 7, 15),), 0),
            (3, 1, 17, 0, 3, ((3, 0, 3, 21),), 0),
        ),
        ((0, 0, 8), (5, 0, 4), (6, 0, 12), (7, 0, 10), (12, 0, 14), (13, 0, 6), (14, 0, 0), (15, 1, 10), (16, 1, 13), (19, 0, 2), (20, 1, 14), (21, 1, 15), (23, 1, 8), (24, 1, 9)),
    ),
    (
        (
            (0, 0, -1, 0, 10, ((0, 0, 10, 2), (1, 0, 10, 3), (5, 0, 10, 3), (3, 0, 10, 0)), 0),
            (7, 0, 20, 1, 3, ((4, 1, 3, 24),), 0),
            (5, 0, 17, 1, 7, ((8, 1, 7, 24),), 0),
            (1, 0, 1, 0, 14, ((3, 0, 14, 6),), 0),
            (1, 0, 2, 0, 6, ((5, 0, 6, 12), (1, 0, 6, 10), (3, 0, 6, 8)), 0),
            (1, 0, 3, 0, 8, ((1, 0, 8, 9), (3, 0, 8, 7)), 0),
            (4, 0, 16, 0, 0, ((3, 0, 0, 21),), 0),
            (5, 0, 18, 2, 0, ((0, 1, 0, 23),), 0),
            (2, 1, 7, 0, 2, ((3, 0, 2, 14),), 0),
            (2, 1, 8, 0, 12, ((0, 0, 12, 16), (3, 0, 12, 15)), 0),
            (2, 1, 9, 0, 4, ((3, 0, 4, 16),), 0),
            (6, 1, 19, 1, 2, ((4, 1, 2, 23),), 0),
            (3, 1, 14, 1, 4, ((4, 1, 4, 17),), 0),
        ),
        ((0, 0, 11), (4, 0, 15), (5, 0, 9), (6, 0, 7), (10, 0, 3), (11, 0, 13), (12, 0, 5), (13, 1, 5), (15, 0, 1), (21, 1, 6), (22, 1, 0), (23, 1, 1)),
    ),
    (
        (
            (0, 0, -1, 0, 11, ((0, 0, 11, 2), (5, 0, 11, 4), (1, 0, 11, 3), (3, 0, 11, 0)), 0),
            (1, 0, 1, 0, 15, ((5, 0, 15, 8), (3, 0, 15, 4)), 0),
            (1, 0, 2, 2, 0, ((0, 1, 11, 7),), 0),
            (1, 0, 3, 0, 7, ((1, 0, 7, 8), (5, 0, 7, 11), (3, 0, 7, 6)), 0),
            (1, 0, 4, 0, 9, ((1, 0, 9, 9), (3, 0, 9, 5)), 0),
            (1, 0, 5, 2, 1, ((8, 2, 0, 9),), 0),
            (5, 0, 22, 1, 14, ((4, 1, 14, 23),), 0),
            (2, 0, 9, 1, 9, ((4, 1, 9, 12), (2, 2, 4, 17)), 0),
            (2, 0, 10, 1, 8, ((8, 1, 8, 15),), 0),
            (2, 1, 11, 0, 3, ((5, 0, 3, 17), (3, 0, 3, 10)), 0),
            (2, 1, 12, 0, 13, ((0, 0, 13, 16), (3, 0, 13, 11)), 0),
            (3, 1, 17, 0, 1, ((3, 0, 1, 15),), 0),
            (3, 1, 18, 1, 12, ((8, 1, 12, 20),), 0),
            (2, 1, 13, 0, 5, ((3, 0, 5, 12),), 0),
            (3, 1, 20, 1, 13, ((4, 1, 13, 20), (8, 1, 13, 21)), 0),
        ),
        ((0, 0, 10), (6, 0, 14), (7, 0, 8), (8, 0, 6), (14, 0, 2), (15, 0, 12), (16, 0, 4), (19, 1, 11), (21, 0, 0), (23, 1, 10), (24, 1, 15)),
    ),
    (
        (
            (0, 0, -1, 0, 12, ((0, 0, 12, 5), (5, 0, 12, 2), (1, 0, 12, 2), (3, 0, 12, 0)), 0),
            (4, 0, 13, 0, 6, ((4, 2, 0, 18), (3, 0, 6, 16)), 0),
            (1, 0, 1, 0, 14, ((0, 0, 14, 9), (1, 0, 14, 9), (3, 0, 14, 3)), 0),
            (4, 0, 14, 2, 1, ((1, 1, 0, 22),), 0),
            (6, 0, 19, 1, 0, ((4, 1, 0, 21),), 0),
            (1, 0, 2, 0, 0, ((5, 0, 0, 7), (2, 2, 0, 9), (3, 0, 0, 4)), 0),
            (1, 0, 3, 0, 8, ((3, 0, 8, 5),), 0),
            (2, 1, 6, 0, 4, ((3, 0, 4, 9),), 0),
            (2, 1, 7, 0, 2, ((3, 0, 2, 10),), 0),
            (6, 1, 20, 1, 1, ((8, 1, 1, 23),), 0),
            (6, 1, 21, 1, 6, ((4, 1, 6, 22),), 0),
            (6, 1, 22, 1, 7, ((4, 1, 7, 23),), 0),
            (2, 1, 8, 2, 0, ((1, 1, 3, 19),), 0),
            (2, 1, 9, 0, 10, ((3, 0, 10, 11),), 0),
        ),
        ((0, 0, 13), (4, 0, 1), (5, 0, 9), (10, 0, 5), (11, 0, 3), (12, 0, 11), (15, 0, 15), (16, 0, 7), (17, 1, 2), (18, 1, 3), (23, 1, 4), (24, 1, 5)),
    ),
    (
        (
            (0, 0, -1, 0, 13, ((4, 2, 0, 2), (1, 0, 13, 3), (5, 0, 13, 2), (0, 0, 13, 3), (3, 0, 13, 0)), 0),
            (5, 0, 19, 2, 2, ((8, 2, 3, 23), (2, 1, 15, 20)), 0),
            (1, 0, 1, 0, 1, ((5, 0, 1, 7), (1, 0, 1, 10), (3, 0, 1, 4)), 0),
            (5, 0, 20, 1, 11, ((2, 2, 1, 22), (8, 1, 11, 25)), 0),
            (1, 0, 2, 0, 9, ((0, 0, 9, 9), (3, 0, 9, 5)), 0),
            (6, 0, 22, 1, 9, ((4, 1, 9, 24),), 0),
            (2, 1, 6, 0, 5, ((3, 0, 5, 10),), 0),
            (2, 1, 7, 0, 3, ((3, 0, 3, 11),), 0),
            (6, 1, 23, 1, 8, ((8, 1, 8, 26),), 0),
            (3, 1, 12, 1, 15, ((5, 2, 0, 18), (8, 1, 15, 17)), 0),
            (2, 1, 8, 0, 11, ((0, 0, 11, 15), (3, 0, 11, 12)), 0),
            (3, 1, 13, 0, 15, ((3, 0, 15, 15),), 0),
            (3, 1, 14, 0, 7, ((3, 0, 7, 16),), 0),
            (4, 1, 17, 2, 1, ((8, 2, 2, 21), (2, 1, 8, 19)), 0),
            (3, 1, 15, 2, 0, ((5, 1, 11, 19),), 0),
        ),
        ((0, 0, 12), (3, 0, 14), (4, 0, 0), (5, 0, 8), (9, 0, 4), (10, 0, 2), (11, 0, 10), (16, 0, 6), (18, 1, 10), (21, 1, 14), (24, 1, 12), (25, 1, 13)),
    ),
    (
        (
            (0, 0, -1, 0, 14, ((5, 0, 14, 1), (0, 0, 14, 1), (1, 0, 14, 1), (3, 0, 14, 0)), 0),
            (1, 0, 1, 0, 2, ((1, 0, 2, 7), (5, 0, 2, 7), (3, 0, 2, 4)), 0),
            (5, 0, 18, 2, 0, ((5, 1, 1, 20),), 0),
            (1, 0, 2, 0, 12, ((0, 0, 12, 8), (1, 0, 12, 8), (3, 0, 12, 5)), 0),
            (5, 1, 19, 1, 4, ((8, 1, 4, 21),), 0),
            (1, 1, 3, 0, 10, ((0, 0, 10, 11), (3, 0, 10, 6)), 0),
            (5, 1, 20, 1, 5, ((8, 1, 5, 22),), 0),
            (2, 1, 7, 0, 0, ((4, 2, 1, 17), (3, 0, 0, 10)), 0),
            (3, 1, 13, 0, 4, ((3, 0, 4, 15),), 0),
            (3, 1, 14, 1, 1, ((8, 1, 1, 18),), 0),
            (2, 1, 9, 0, 8, ((3, 0, 8, 11),), 0),
            (2, 1, 10, 0, 6, ((3, 0, 6, 12),), 0),
        ),
        ((0, 0, 15), (4, 0, 3), (5, 0, 13), (6, 0, 11), (8, 0, 1), (11, 0, 7), (12, 0, 9), (15, 1, 0), (16, 0, 5), (17, 1, 2), (21, 1, 6), (22, 1, 7), (23, 1, 3)),
    ),
    (
        (
            (0, 0, -1, 0, 15, ((0, 0, 15, 1), (2, 2, 0, 2), (1, 0, 15, 1), (3, 0, 15, 0)), 0),
            (5, 0, 16, 1, 12, ((8, 1, 12, 21),), 0),
            (4, 0, 14, 0, 5, ((3, 0, 5, 16),), 0),
            (5, 0, 18, 2, 0, ((2, 1, 15, 22),), 0),
            (1, 0, 1, 0, 3, ((7, 2, 0, 7), (3, 0, 3, 4)), 0),
            (5, 0, 20, 2, 1, ((4, 2, 1, 22), (5, 1, 9, 22)), 0),
            (6, 0, 21, 2, 2, ((2, 1, 10, 23),), 0),
            (1, 0, 2, 0, 13, ((2, 2, 2, 9), (3, 0, 13, 5)), 0),
            (6, 0, 22, 1, 14, ((4, 1, 14, 23),), 0),
            (1, 0, 3, 0, 11, ((3, 0, 11, 6),), 0),
            (6, 0, 23, 2, 3, ((2, 1, 13, 25),), 0),
            (2, 0, 7, 0, 1, ((0, 0, 1, 13), (1, 0, 1, 17), (3, 0, 1, 8)), 0),
            (2, 1, 8, 0, 7, ((5, 0, 7, 14), (3, 0, 7, 11)), 0),
            (6, 1, 24, 1, 15, ((4, 1, 15, 24), (8, 1, 15, 25)), 0),
            (2, 1, 9, 0, 9, ((0, 0, 9, 17), (3, 0, 9, 12)), 0),
            (3, 1, 13, 1, 8, ((5, 2, 1, 17), (8, 1, 8, 18)), 0),
        ),
        ((0, 0, 14), (4, 0, 2), (5, 0, 12), (6, 0, 10), (10, 0, 0), (11, 0, 8), (12, 0, 6), (15, 0, 4), (17, 1, 13), (19, 1, 11), (25, 1, 9), (26, 1, 10)),
    ),
)
VMEM_LIMIT = 27 << 20
MBV, NBV = 512, 1024
LAST = 2

F32, BF16 = jnp.float32, jnp.bfloat16
MESH = pl.DeviceIdType.MESH
NT_PTS = 3
PAIRS, ROWS, COLS, OWN = 2048, 2048, 1024, 128
KC = PAIRS // NC
KK = 512
NK = PAIRS // KK
PER = KK // KC
MB, NB = MBV, NBV
NM = ROWS // MB
MB2 = 512
NM2 = ROWS // MB2
EARLY = NK - LAST
START = SMAX + PER
STEPS = NC + SMAX


def flip(value, bits):
    return [jnp.int32(b) * (1 - 2 * ((value // b) % 2)) for b in bits]


def flipped(value, deltas, bits, mask):
    for delta, bit in zip(deltas, bits):
        if mask & bit:
            value = value + delta
    return value


def weigh(x, factor, w_ref):
    rows, x = x.shape[0], x.astype(F32)
    for t in range(NT_PTS):
        w_ref[pl.ds(t * rows, rows), :] = (x * factor(t)).astype(BF16)


def product(w, y):
    return lax.dot_general(w, y, (((1,), (1,)), ((), ())), preferred_element_type=F32)


def gather_kernel(points, weights, own_ref, den_ref, acc, x_ref, y_ref, f_ref,
                  transit, w_ref, send_sem, recv_sem, local_sem):
    row, col = lax.axis_index("row"), lax.axis_index("col")
    row_d, col_d = flip(row, (1, 2, 4)), flip(col, (1, 2, 4, 8))
    peers = [
        {"row": flipped(row, row_d, (1, 2, 4), dr), "col": flipped(col, col_d, (1, 2, 4, 8), dc)}
        for dr, dc in TARGETS
    ]
    barrier = pltpu.get_barrier_semaphore()
    for peer in peers:
        pl.semaphore_signal(barrier, inc=1, device_id=peer, device_id_type=MESH)

    high = row // 4
    code = row * 2 + high
    code_d = flip(code, (1, 2, 4, 8))

    def lanes(j):
        return pl.ds(pl.multiple_of((j % PER) * KC, KC), KC)

    def place(kind, mark, j):
        if kind == 2:
            return transit.at[j, mark]
        slot = flipped(code, code_d, (1, 2, 4, 8), mark)
        if kind == 0:
            return x_ref.at[j // PER, pl.ds(pl.multiple_of(slot * OWN, OWN), OWN), lanes(j)]
        slot = slot % 8
        return y_ref.at[j // PER, pl.ds(pl.multiple_of(slot * OWN, OWN), OWN), lanes(j)]

    for k in range(NK):
        x_ref[k, pl.ds(pl.multiple_of(col * OWN, OWN), OWN), :] = own_ref[pl.ds(k * KK, KK), :].T
    for t in range(NT_PTS):
        f_ref[t, :] = weights[t] * jnp.exp(-points[t] * den_ref[...])
    pl.semaphore_wait(barrier, len(TARGETS))

    k_col = col // 2
    bits = [((row // b) % 2 + (k_col // b) % 2) % 2 for b in (4, 2, 1)]
    which = (bits[0] * 4 + bits[1] * 2 + bits[2]) * 2 + ((col % 2) + high) % 2

    def arrived(kind, mark, event, j):
        ref = place(kind, mark, j)
        pltpu.make_async_copy(ref, ref, recv_sem.at[j, event]).wait()

    def act(action, j):
        _, _, event, kind, mark, kids, local = action
        if event >= 0:
            arrived(kind, mark, event, j)
        src = place(kind, mark, j)
        for target, to_kind, to_mark, to_event in kids:
            pltpu.make_async_remote_copy(
                src_ref=src, dst_ref=place(to_kind, to_mark, j),
                send_sem=send_sem.at[j], recv_sem=recv_sem.at[j, to_event],
                device_id=peers[target], device_id_type=MESH,
            ).start()
        if local:
            pltpu.make_async_copy(src, place(1, mark, j), local_sem.at[j]).start()

    def bulk_wait(sem, copies):
        ref = acc.at[0, pl.ds(0, copies * OWN * KC // (2 * COLS)), :]
        pltpu.make_async_copy(ref, ref, sem).wait()

    def choose(run, low, high):
        if high - low == 1:
            run(low)
            return
        middle = (low + high) // 2
        pl.when(which < middle)(lambda: choose(run, low, middle))
        pl.when(which >= middle)(lambda: choose(run, middle, high))

    def settle(j):
        def run(g):
            actions, last = PROGRAMS[g]
            for event, kind, mark in last:
                arrived(kind, mark, event, j)
            copies = sum(a[6] for a in actions)
            if copies:
                bulk_wait(local_sem.at[j], copies)

        choose(run, 0, len(PROGRAMS))

    def block(k, m):
        rows = pl.ds(pl.multiple_of(m * MB, MB), MB)
        weigh(x_ref[k, rows, :], lambda t: f_ref[pl.ds(t, 1), pl.ds(pl.multiple_of(k * KK, KK), KK)], w_ref)

        @pl.loop(0, COLS // NB)
        def _(n):
            at = pl.ds(pl.multiple_of(n * NB, NB), NB)
            for t in range(NT_PTS):
                acc[t, rows, at] += product(w_ref[pl.ds(t * MB, MB), :], y_ref[k, at, :])

    @pl.loop(0, STEPS)
    def _(p):
        k = jnp.maximum(p - START, 0) // PER
        part = jnp.maximum(p - START, 0) % PER
        busy = jnp.logical_and(p >= START, p < START + EARLY * PER)

        @pl.when(jnp.logical_and(busy, part == 0))
        def _():
            for i in range(PER):
                settle(k * PER + i)

        @pl.loop(0, NG)
        def _(group):
            def run(g):
                for at in range(NG):
                    mine = [a for a in PROGRAMS[g][0] if a[1] == at]

                    def go(mine=mine):
                        for lag, same in itertools.groupby(mine, lambda a: a[0]):
                            @pl.when(jnp.logical_and(p >= lag, p < NC + lag))
                            def _(lag=lag, same=tuple(same)):
                                for a in same:
                                    act(a, p - lag)
                    if NG > 1:
                        pl.when(group == at)(go)
                    else:
                        go()

            choose(run, 0, len(PROGRAMS))

            if not EARLY:
                return

            @pl.when(jnp.logical_and(p == 0, group == 0))
            def _():
                @pl.loop(0, ROWS // 64)
                def _(m):
                    at = pl.ds(pl.multiple_of(m * 64, 64), 64)
                    acc[:, at, :] = jnp.zeros((NT_PTS, 64, COLS), F32)

            @pl.when(busy)
            def _():
                for b in range(NM // PER // NG):
                    block(k, (part * NG + group) * (NM // PER // NG) + b)

    @pl.loop(NC - PER * LAST, NC)
    def _(j):
        settle(j)

    def sent(g):
        @pl.loop(0, NC)
        def _(j):
            bulk_wait(send_sem.at[j], sum(len(a[5]) for a in PROGRAMS[g][0]))

    choose(sent, 0, len(PROGRAMS))


def last_kernel(acc, x_ref, y_ref, f_ref, out, w_ref, buf, sem):
    def copy(m, slot):
        return pltpu.make_async_copy(
            buf.at[slot], out.at[:, pl.ds(pl.multiple_of(m * MB2, MB2), MB2), :], sem.at[slot]
        )

    @pl.loop(0, NM2)
    def _(m):
        slot = m % 2
        rows = pl.ds(pl.multiple_of(m * MB2, MB2), MB2)

        @pl.when(m >= 2)
        def _():
            copy(m - 2, slot).wait()

        for k in range(EARLY, NK):
            at = slice(k * KK, (k + 1) * KK)
            weigh(x_ref[k, rows, :], lambda t: f_ref[t:t + 1, at], w_ref)
            for t in range(NT_PTS):
                d = product(w_ref[pl.ds(t * MB2, MB2), :], y_ref[k])
                if k > EARLY:
                    d += buf[slot, t]
                elif EARLY:
                    d += acc[t, rows, :]
                buf[slot, t] = d
        copy(m, slot).start()

    copy(NM2 - 2, (NM2 - 2) % 2).wait()
    copy(NM2 - 1, (NM2 - 1) % 2).wait()


def on_device(pair_ints, denominators, lap_points, lap_weights):
    vmem = pl.BlockSpec(memory_space=pltpu.VMEM)
    smem = pl.BlockSpec(memory_space=pltpu.SMEM)
    held = pl.pallas_call(
        gather_kernel,
        out_shape=(
            pltpu.VMEM((NT_PTS, ROWS, COLS), F32),
            pltpu.VMEM((NK, ROWS, KK), BF16),
            pltpu.VMEM((NK, COLS, KK), BF16),
            pltpu.VMEM((NT_PTS, PAIRS), F32),
        ),
        in_specs=[smem, smem, vmem, vmem],
        out_specs=(vmem,) * 4,
        scratch_shapes=[
            pltpu.VMEM((NC, NT, OWN, KC), BF16),
            pltpu.VMEM((NT_PTS * MB, KK), BF16),
            pltpu.SemaphoreType.DMA((NC,)),
            pltpu.SemaphoreType.DMA((NC, NE)),
            pltpu.SemaphoreType.DMA((NC,)),
        ],
        compiler_params=pltpu.CompilerParams(
            collective_id=0, has_side_effects=True, vmem_limit_bytes=VMEM_LIMIT
        ),
    )(lap_points, lap_weights, pair_ints, denominators)
    held = [pltpu.with_memory_space_constraint(a, pltpu.VMEM) for a in held]
    return pl.pallas_call(
        last_kernel,
        out_shape=jax.ShapeDtypeStruct((NT_PTS, ROWS, COLS), F32),
        in_specs=[vmem] * 4,
        out_specs=pl.BlockSpec(memory_space=pl.ANY),
        scratch_shapes=[
            pltpu.VMEM((NT_PTS * MB2, KK), BF16),
            pltpu.VMEM((2, NT_PTS, MB2, COLS), F32),
            pltpu.SemaphoreType.DMA((2,)),
        ],
        compiler_params=pltpu.CompilerParams(vmem_limit_bytes=VMEM_LIMIT),
    )(*held)


def solution(mesh):
    in_specs = (P(None, ("row", "col")), P(), P(), P())
    out_specs = P(None, "row", "col")
    return jax.shard_map(
        on_device, mesh=mesh, in_specs=in_specs, out_specs=out_specs, check_vma=False
    )
```

time: 197 us -> 82.8 us (0.42); the launches traced: 194 us -> 82.7 us
  waiting for transfers between devices: 89.6 us -> 0 us
  Pallas kernels: 0 us -> 82.5 us
  blocking collectives: 42 us -> 0 us
  matrix products: 33.6 us -> 0 us
  local copies, waits for them, and re-layouts: 13.7 us -> 0 us
  between operations: 13.4 us -> 0.17 us
    all_gather x2 -> x0, waiting for transfers between devices: 88.9 us -> none  [the longest x1 58.4 us: on_device(): col_whole = lax.all_gather(col_block, 'row', axis=0, tiled=True)]
    pallas_call x0 -> x2, Pallas kernels: none -> 82.5 us  [the longest x1 65.9 us: on_device(): pl.pallas_call(gather_kernel, out_shape=(pltpu.VMEM((NT_PTS, ROWS, COLS),...]
    all_to_all x2 -> x0, blocking collectives: 42 us -> none  [the longest x1 23 us: on_device(): lax.all_to_all(pair_ints, ('row', 'col'), split_axis=0, concat_axis=1, ti...]
    dot_general x1 -> x0, matrix products: 33.6 us -> none  [on_device(): jnp.einsum('trp,rq->tpq', weighted, col_whole, preferred_element_type=jnp...]
    convert_element_type x1 -> x0, local copies, waits for them, and re-layouts: 13 us -> none  [on_device(): lax.all_gather(pair_ints, 'col', axis=1, tiled=True).astype(jnp.float32)]
  transfers between devices with their start and end apart: 2 -> 0, of which waited for: 2 -> 0; matrix products, arithmetic and copies ran while one was open for 8% -> 0% of each run, Pallas kernels for 0% -> 0%
where the time goes in v3:
time: 82.8 us; the launch traced here: 82.7 us
  Pallas kernels  82.5 us (100%)
    pallas_call x1, Pallas kernels, on_device(): pl.pallas_call(gather_kernel, out_shape=(pltpu.VMEM((NT_PTS, ROWS, COLS),...  65.9 us
    pallas_call x1, Pallas kernels, on_device(): pl.pallas_call(last_kernel, out_shape=jax.ShapeDtypeStruct((NT_PTS, ROWS,...  16.6 us

profile of v3, /device:TPU:36, one launch (start us, length us, event | category | flops | bytes accessed | tf_op | source)
XLA Modules:
  0.0 82.7 jit_solution(13971102557114300267)
XLA Ops:
  0.0 65.9 %shard_map.46 = (f32[3,2048,1024]{2,1,0:T(8,128)S(1)}, bf16[4,2048,512]{2,1,0:T(8,128)(2,1)S(1)}, bf16[4,1024,512]{2,1,0:T(8,128)(2,1)S(1)}, f32[3,2048]{1,0:T(4,128)S(1)}) custom-call(f32[3]{0:T(128)} %points.1, f32[3]{0:T(128)} %weights.1, bf16[2048,128]{1,0:T(8,128)(2,1)} %own_ref.1, f32[2048]{0:T(1024)} %den_ref.1), custom_call_target="tpu_custom_call" | custom-call | tf_op jit(solution)/shard_map/pallas_call | solution.py:542
  65.9 16.6 %shard_map.47 = f32[3,2048,1024]{2,1,0:T(8,128)} custom-call(f32[3,2048,1024]{2,1,0:T(8,128)S(1)} %get-tuple-element.9.acc, bf16[4,2048,512]{2,1,0:T(8,128)(2,1)S(1)} %get-tuple-element.10.x_ref, bf16[4,1024,512]{2,1,0:T(8,128)(2,1)S(1)} %get-tuple-element.11.y_ref, f32[3,2048]{1,0:T(4,128)S(1)} %get-tuple-element.12.f_ref), custom_call_target="tpu_custom_call" | custom-call | tf_op jit(solution)/shard_map/pallas_call | solution.py:564

commit v4 on v3

--- a/solution.py
+++ b/solution.py
@@ -7,7 +7,7 @@
 from jax.experimental.pallas import tpu as pltpu
 from jax.sharding import PartitionSpec as P
 
-NC, NG, SMAX, NT, NE = 8, 2, 8, 6, 27
+NC, NG, SMAX, NT, NE = 8, 1, 8, 6, 27
 TARGETS = ((0, 12), (0, 4), (4, 2), (0, 1), (3, 0), (0, 2), (1, 1), (3, 1), (1, 0), (4, 3))
 PROGRAMS = (
     (
@@ -25,11 +25,11 @@
             (0, 0, 0, 0, 1, (), 1),
             (2, 0, 11, 0, 6, ((3, 0, 6, 11),), 1),
             (1, 0, 6, 0, 5, (), 1),
-            (2, 1, 12, 0, 8, ((3, 0, 8, 12),), 0),
-            (3, 1, 17, 2, 4, ((5, 1, 0, 22),), 0),
-            (2, 1, 13, 2, 3, ((2, 1, 4, 20), (5, 1, 4, 17)), 0),
-            (1, 1, 8, 0, 3, (), 1),
-            (4, 1, 20, 2, 5, ((2, 1, 3, 23),), 0),
+            (2, 0, 12, 0, 8, ((3, 0, 8, 12),), 0),
+            (3, 0, 17, 2, 4, ((5, 1, 0, 22),), 0),
+            (2, 0, 13, 2, 3, ((2, 1, 4, 20), (5, 1, 4, 17)), 0),
+            (1, 0, 8, 0, 3, (), 1),
+            (4, 0, 20, 2, 5, ((2, 1, 3, 23),), 0),
         ),
         ((7, 0, 13), (14, 0, 15), (16, 0, 9), (19, 0, 11)),
     ),
@@ -41,14 +41,14 @@
             (1, 0, 2, 0, 3, ((1, 0, 3, 8), (0, 0, 3, 7), (7, 1, 3, 9), (3, 0, 3, 8)), 0),
             (1, 0, 3, 0, 13, ((5, 0, 13, 5), (3, 0, 13, 7)), 1),
             (2, 0, 7, 0, 15, ((4, 1, 15, 15), (0, 0, 15, 13), (3, 0, 15, 14)), 1),
-            (4, 1, 16, 0, 10, (), 1),
-            (2, 1, 8, 0, 7, ((3, 0, 7, 15),), 0),
-            (2, 1, 9, 0, 9, ((8, 1, 9, 16), (3, 0, 9, 16)), 1),
-            (3, 1, 13, 2, 0, ((0, 2, 2, 19),), 0),
-            (3, 1, 14, 2, 1, ((2, 1, 14, 17),), 0),
-            (2, 1, 10, 0, 14, (), 1),
-            (1, 1, 5, 0, 12, (), 1),
-            (3, 1, 15, 0, 11, ((4, 1, 11, 20), (8, 1, 11, 22), (3, 0, 11, 19)), 1),
+            (4, 0, 16, 0, 10, (), 1),
+            (2, 0, 8, 0, 7, ((3, 0, 7, 15),), 0),
+            (2, 0, 9, 0, 9, ((8, 1, 9, 16), (3, 0, 9, 16)), 1),
+            (3, 0, 13, 2, 0, ((0, 2, 2, 19),), 0),
+            (3, 0, 14, 2, 1, ((2, 1, 14, 17),), 0),
+            (2, 0, 10, 0, 14, (), 1),
+            (1, 0, 5, 0, 12, (), 1),
+            (3, 0, 15, 0, 11, ((4, 1, 11, 20), (8, 1, 11, 22), (3, 0, 11, 19)), 1),
         ),
         ((0, 0, 0), (4, 0, 4), (6, 0, 2), (11, 0, 6)),
     ),
@@ -61,10 +61,10 @@
             (4, 0, 20, 0, 8, ((9, 1, 8, 23), (3, 0, 8, 18)), 0),
             (4, 0, 21, 0, 0, ((3, 0, 0, 19),), 0),
             (2, 0, 7, 0, 4, ((0, 0, 4, 13), (2, 1, 4, 16), (3, 0, 4, 10)), 0),
-            (2, 1, 8, 0, 12, ((6, 2, 1, 14), (3, 0, 12, 11)), 0),
-            (2, 1, 9, 1, 1, ((4, 1, 1, 19),), 0),
-            (2, 1, 10, 2, 0, ((1, 1, 7, 17),), 0),
-            (2, 1, 11, 0, 10, ((5, 0, 10, 18), (3, 0, 10, 12)), 0),
+            (2, 0, 8, 0, 12, ((6, 2, 1, 14), (3, 0, 12, 11)), 0),
+            (2, 0, 9, 1, 1, ((4, 1, 1, 19),), 0),
+            (2, 0, 10, 2, 0, ((1, 1, 7, 17),), 0),
+            (2, 0, 11, 0, 10, ((5, 0, 10, 18), (3, 0, 10, 12)), 0),
         ),
         ((0, 0, 3), (2, 1, 3), (4, 0, 15), (5, 0, 7), (12, 0, 13), (13, 0, 11), (14, 0, 5), (15, 1, 2), (16, 1, 5), (17, 1, 4), (18, 0, 1), (19, 0, 9), (22, 1, 0), (23, 1, 6)),
     ),
@@ -74,16 +74,16 @@
             (1, 0, 1, 0, 15, ((5, 0, 15, 7), (1, 0, 15, 8), (3, 0, 15, 4)), 0),
             (1, 0, 2, 0, 7, ((6, 2, 2, 10), (5, 0, 7, 8), (3, 0, 7, 5)), 0),
             (5, 0, 21, 2, 2, ((0, 1, 15, 24),), 0),
-            (2, 1, 5, 0, 13, ((3, 0, 13, 12),), 0),
-            (3, 1, 13, 0, 1, ((7, 2, 3, 21), (6, 2, 5, 20), (3, 0, 1, 18)), 0),
-            (3, 1, 14, 2, 1, ((0, 1, 12, 16),), 0),
-            (2, 1, 6, 1, 14, ((4, 1, 14, 16),), 0),
-            (2, 1, 7, 2, 0, ((1, 1, 14, 17),), 0),
-            (2, 1, 8, 0, 11, ((2, 1, 11, 18), (3, 0, 11, 13)), 0),
-            (3, 1, 15, 1, 12, ((4, 1, 12, 19),), 0),
-            (2, 1, 9, 0, 5, ((9, 1, 5, 18), (0, 0, 5, 14), (3, 0, 5, 14)), 0),
-            (3, 1, 16, 1, 11, ((4, 1, 11, 20),), 0),
-            (3, 1, 17, 0, 9, ((3, 0, 9, 19),), 0),
+            (2, 0, 5, 0, 13, ((3, 0, 13, 12),), 0),
+            (3, 0, 13, 0, 1, ((7, 2, 3, 21), (6, 2, 5, 20), (3, 0, 1, 18)), 0),
+            (3, 0, 14, 2, 1, ((0, 1, 12, 16),), 0),
+            (2, 0, 6, 1, 14, ((4, 1, 14, 16),), 0),
+            (2, 0, 7, 2, 0, ((1, 1, 14, 17),), 0),
+            (2, 0, 8, 0, 11, ((2, 1, 11, 18), (3, 0, 11, 13)), 0),
+            (3, 0, 15, 1, 12, ((4, 1, 12, 19),), 0),
+            (2, 0, 9, 0, 5, ((9, 1, 5, 18), (0, 0, 5, 14), (3, 0, 5, 14)), 0),
+            (3, 0, 16, 1, 11, ((4, 1, 11, 20),), 0),
+            (3, 0, 17, 0, 9, ((3, 0, 9, 19),), 0),
         ),
         ((0, 0, 2), (3, 0, 14), (4, 0, 6), (10, 0, 4), (11, 0, 12), (12, 0, 10), (18, 0, 8), (19, 0, 0), (20, 1, 15), (22, 1, 9), (23, 1, 13), (24, 1, 10), (25, 1, 8)),
     ),
@@ -98,11 +98,11 @@
             (2, 0, 8, 2, 1, ((2, 1, 1, 13),), 0),
             (6, 0, 22, 1, 6, ((8, 1, 6, 24),), 0),
             (1, 0, 3, 0, 8, ((5, 0, 8, 12), (7, 2, 0, 7), (1, 0, 8, 12), (3, 0, 8, 5)), 0),
-            (2, 1, 9, 2, 2, ((0, 1, 4, 16),), 0),
-            (1, 1, 5, 0, 0, ((5, 0, 0, 13), (0, 0, 0, 13), (3, 0, 0, 6)), 0),
-            (3, 1, 17, 0, 14, ((3, 0, 14, 17),), 0),
-            (3, 1, 18, 1, 0, ((2, 2, 1, 20),), 0),
-            (2, 1, 10, 0, 12, ((3, 0, 12, 10),), 0),
+            (2, 0, 9, 2, 2, ((0, 1, 4, 16),), 0),
+            (1, 0, 5, 0, 0, ((5, 0, 0, 13), (0, 0, 0, 13), (3, 0, 0, 6)), 0),
+            (3, 0, 17, 0, 14, ((3, 0, 14, 17),), 0),
+            (3, 0, 18, 1, 0, ((2, 2, 1, 20),), 0),
+            (2, 0, 10, 0, 12, ((3, 0, 12, 10),), 0),
         ),
         ((0, 0, 5), (4, 0, 7), (6, 0, 9), (7, 0, 1), (13, 0, 13), (14, 0, 3), (15, 0, 11), (16, 1, 1), (19, 1, 7), (20, 0, 15), (23, 1, 3), (24, 1, 5), (25, 1, 4), (26, 1, 2)),
     ),
@@ -116,14 +116,14 @@
             (1, 0, 2, 0, 9, ((5, 0, 9, 10), (3, 0, 9, 6)), 0),
             (5, 0, 20, 1, 13, ((8, 1, 13, 24),), 0),
             (1, 0, 3, 0, 1, ((7, 2, 0, 10), (5, 0, 1, 11), (3, 0, 1, 7)), 0),
-            (5, 1, 21, 1, 12, ((4, 1, 12, 24),), 0),
-            (2, 1, 7, 0, 13, ((3, 0, 13, 13),), 0),
-            (3, 1, 13, 2, 0, ((8, 2, 1, 19), (2, 1, 11, 17)), 0),
-            (3, 1, 14, 1, 9, ((4, 1, 9, 20),), 0),
-            (2, 1, 8, 0, 3, ((3, 0, 3, 14),), 0),
-            (6, 1, 23, 1, 14, ((4, 1, 14, 25),), 0),
-            (2, 1, 9, 0, 11, ((3, 0, 11, 15),), 0),
-            (3, 1, 15, 0, 15, ((3, 0, 15, 20),), 0),
+            (5, 0, 21, 1, 12, ((4, 1, 12, 24),), 0),
+            (2, 0, 7, 0, 13, ((3, 0, 13, 13),), 0),
+            (3, 0, 13, 2, 0, ((8, 2, 1, 19), (2, 1, 11, 17)), 0),
+            (3, 0, 14, 1, 9, ((4, 1, 9, 20),), 0),
+            (2, 0, 8, 0, 3, ((3, 0, 3, 14),), 0),
+            (6, 0, 23, 1, 14, ((4, 1, 14, 25),), 0),
+            (2, 0, 9, 0, 11, ((3, 0, 11, 15),), 0),
+            (3, 0, 15, 0, 15, ((3, 0, 15, 20),), 0),
         ),
         ((0, 0, 4), (4, 0, 6), (5, 0, 8), (6, 0, 0), (10, 0, 12), (11, 0, 2), (12, 0, 10), (17, 0, 14), (22, 1, 15)),
     ),
@@ -135,11 +135,11 @@
             (3, 0, 13, 0, 0, ((0, 0, 0, 16), (1, 0, 0, 21), (3, 0, 0, 14)), 0),
             (6, 0, 21, 2, 0, ((2, 1, 5, 24), (5, 1, 5, 24)), 0),
             (1, 0, 1, 0, 2, ((3, 0, 2, 4),), 0),
-            (6, 1, 22, 2, 1, ((5, 1, 2, 26),), 0),
-            (1, 1, 2, 0, 10, ((9, 2, 0, 8), (3, 0, 10, 5)), 0),
-            (1, 1, 3, 0, 4, ((3, 0, 4, 6),), 0),
-            (2, 1, 8, 1, 2, ((8, 1, 2, 18), (2, 2, 0, 15)), 0),
-            (2, 1, 10, 0, 14, ((3, 0, 14, 12),), 0),
+            (6, 0, 22, 2, 1, ((5, 1, 2, 26),), 0),
+            (1, 0, 2, 0, 10, ((9, 2, 0, 8), (3, 0, 10, 5)), 0),
+            (1, 0, 3, 0, 4, ((3, 0, 4, 6),), 0),
+            (2, 0, 8, 1, 2, ((8, 1, 2, 18), (2, 2, 0, 15)), 0),
+            (2, 0, 10, 0, 14, ((3, 0, 14, 12),), 0),
         ),
         ((0, 0, 7), (4, 0, 3), (5, 0, 11), (6, 0, 5), (7, 1, 3), (9, 1, 5), (11, 0, 15), (14, 0, 9), (15, 0, 1), (17, 1, 7), (18, 0, 13), (19, 1, 1), (20, 1, 6), (23, 1, 0), (24, 1, 4)),
     ),
@@ -154,12 +154,12 @@
             (2, 0, 7, 1, 11, ((5, 2, 0, 13), (8, 1, 11, 14)), 0),
             (1, 0, 3, 0, 5, ((1, 0, 5, 9), (0, 0, 5, 13), (3, 0, 5, 6)), 0),
             (5, 0, 22, 1, 12, ((8, 1, 12, 23),), 0),
-            (2, 1, 8, 0, 15, ((5, 0, 15, 15), (3, 0, 15, 11)), 0),
-            (2, 1, 9, 2, 0, ((4, 2, 0, 13),), 0),
-            (2, 1, 10, 0, 9, ((2, 2, 1, 14), (3, 0, 9, 14)), 0),
-            (2, 1, 11, 0, 1, ((3, 0, 1, 15),), 0),
-            (3, 1, 15, 1, 9, ((8, 1, 9, 18),), 0),
-            (4, 1, 19, 2, 1, ((2, 1, 9, 19),), 0),
+            (2, 0, 8, 0, 15, ((5, 0, 15, 15), (3, 0, 15, 11)), 0),
+            (2, 0, 9, 2, 0, ((4, 2, 0, 13),), 0),
+            (2, 0, 10, 0, 9, ((2, 2, 1, 14), (3, 0, 9, 14)), 0),
+            (2, 0, 11, 0, 1, ((3, 0, 1, 15),), 0),
+            (3, 0, 15, 1, 9, ((8, 1, 9, 18),), 0),
+            (4, 0, 19, 2, 1, ((2, 1, 9, 19),), 0),
         ),
         ((0, 0, 6), (4, 0, 2), (5, 0, 10), (6, 0, 4), (12, 0, 14), (13, 0, 8), (14, 0, 0), (18, 0, 12), (21, 1, 10), (23, 1, 8), (24, 1, 15)),
     ),
@@ -173,14 +173,14 @@
             (2, 0, 7, 2, 0, ((2, 2, 1, 14),), 0),
             (1, 0, 1, 0, 4, ((5, 0, 4, 9), (3, 0, 4, 5)), 0),
             (5, 0, 22, 1, 0, ((8, 1, 0, 19), (4, 1, 0, 21)), 0),
-            (1, 1, 2, 0, 12, ((3, 0, 12, 6),), 0),
-            (2, 1, 8, 1, 6, ((8, 1, 6, 14), (4, 1, 6, 15)), 0),
-            (2, 1, 9, 0, 14, ((0, 0, 14, 17), (3, 0, 14, 12)), 0),
-            (1, 1, 3, 0, 10, ((1, 0, 10, 9), (0, 0, 10, 12), (3, 0, 10, 7)), 0),
-            (2, 1, 10, 1, 7, ((4, 1, 7, 14), (8, 1, 7, 13)), 0),
-            (5, 1, 23, 1, 1, ((8, 1, 1, 20), (4, 1, 1, 22)), 0),
-            (2, 1, 12, 0, 6, ((1, 0, 6, 13), (3, 0, 6, 13)), 0),
-            (2, 1, 13, 0, 0, ((3, 0, 0, 14),), 0),
+            (1, 0, 2, 0, 12, ((3, 0, 12, 6),), 0),
+            (2, 0, 8, 1, 6, ((8, 1, 6, 14), (4, 1, 6, 15)), 0),
+            (2, 0, 9, 0, 14, ((0, 0, 14, 17), (3, 0, 14, 12)), 0),
+            (1, 0, 3, 0, 10, ((1, 0, 10, 9), (0, 0, 10, 12), (3, 0, 10, 7)), 0),
+            (2, 0, 10, 1, 7, ((4, 1, 7, 14), (8, 1, 7, 13)), 0),
+            (5, 0, 23, 1, 1, ((8, 1, 1, 20), (4, 1, 1, 22)), 0),
+            (2, 0, 12, 0, 6, ((1, 0, 6, 13), (3, 0, 6, 13)), 0),
+            (2, 0, 13, 0, 0, ((3, 0, 0, 14),), 0),
         ),
         ((0, 0, 9), (4, 0, 5), (5, 0, 13), (6, 0, 11), (11, 0, 15), (14, 0, 1), (15, 0, 7), (16, 1, 4), (21, 0, 3), (24, 1, 5)),
     ),
@@ -197,7 +197,7 @@
             (2, 0, 10, 0, 1, ((3, 0, 1, 14),), 0),
             (6, 0, 22, 2, 1, ((2, 1, 15, 23),), 0),
             (2, 0, 11, 0, 7, ((3, 0, 7, 15),), 0),
-            (3, 1, 17, 0, 3, ((3, 0, 3, 21),), 0),
+            (3, 0, 17, 0, 3, ((3, 0, 3, 21),), 0),
         ),
         ((0, 0, 8), (5, 0, 4), (6, 0, 12), (7, 0, 10), (12, 0, 14), (13, 0, 6), (14, 0, 0), (15, 1, 10), (16, 1, 13), (19, 0, 2), (20, 1, 14), (21, 1, 15), (23, 1, 8), (24, 1, 9)),
     ),
@@ -211,11 +211,11 @@
             (1, 0, 3, 0, 8, ((1, 0, 8, 9), (3, 0, 8, 7)), 0),
             (4, 0, 16, 0, 0, ((3, 0, 0, 21),), 0),
             (5, 0, 18, 2, 0, ((0, 1, 0, 23),), 0),
-            (2, 1, 7, 0, 2, ((3, 0, 2, 14),), 0),
-            (2, 1, 8, 0, 12, ((0, 0, 12, 16), (3, 0, 12, 15)), 0),
-            (2, 1, 9, 0, 4, ((3, 0, 4, 16),), 0),
-            (6, 1, 19, 1, 2, ((4, 1, 2, 23),), 0),
-            (3, 1, 14, 1, 4, ((4, 1, 4, 17),), 0),
+            (2, 0, 7, 0, 2, ((3, 0, 2, 14),), 0),
+            (2, 0, 8, 0, 12, ((0, 0, 12, 16), (3, 0, 12, 15)), 0),
+            (2, 0, 9, 0, 4, ((3, 0, 4, 16),), 0),
+            (6, 0, 19, 1, 2, ((4, 1, 2, 23),), 0),
+            (3, 0, 14, 1, 4, ((4, 1, 4, 17),), 0),
         ),
         ((0, 0, 11), (4, 0, 15), (5, 0, 9), (6, 0, 7), (10, 0, 3), (11, 0, 13), (12, 0, 5), (13, 1, 5), (15, 0, 1), (21, 1, 6), (22, 1, 0), (23, 1, 1)),
     ),
@@ -230,12 +230,12 @@
             (5, 0, 22, 1, 14, ((4, 1, 14, 23),), 0),
             (2, 0, 9, 1, 9, ((4, 1, 9, 12), (2, 2, 4, 17)), 0),
             (2, 0, 10, 1, 8, ((8, 1, 8, 15),), 0),
-            (2, 1, 11, 0, 3, ((5, 0, 3, 17), (3, 0, 3, 10)), 0),
-            (2, 1, 12, 0, 13, ((0, 0, 13, 16), (3, 0, 13, 11)), 0),
-            (3, 1, 17, 0, 1, ((3, 0, 1, 15),), 0),
-            (3, 1, 18, 1, 12, ((8, 1, 12, 20),), 0),
-            (2, 1, 13, 0, 5, ((3, 0, 5, 12),), 0),
-            (3, 1, 20, 1, 13, ((4, 1, 13, 20), (8, 1, 13, 21)), 0),
+            (2, 0, 11, 0, 3, ((5, 0, 3, 17), (3, 0, 3, 10)), 0),
+            (2, 0, 12, 0, 13, ((0, 0, 13, 16), (3, 0, 13, 11)), 0),
+            (3, 0, 17, 0, 1, ((3, 0, 1, 15),), 0),
+            (3, 0, 18, 1, 12, ((8, 1, 12, 20),), 0),
+            (2, 0, 13, 0, 5, ((3, 0, 5, 12),), 0),
+            (3, 0, 20, 1, 13, ((4, 1, 13, 20), (8, 1, 13, 21)), 0),
         ),
         ((0, 0, 10), (6, 0, 14), (7, 0, 8), (8, 0, 6), (14, 0, 2), (15, 0, 12), (16, 0, 4), (19, 1, 11), (21, 0, 0), (23, 1, 10), (24, 1, 15)),
     ),
@@ -248,13 +248,13 @@
             (6, 0, 19, 1, 0, ((4, 1, 0, 21),), 0),
             (1, 0, 2, 0, 0, ((5, 0, 0, 7), (2, 2, 0, 9), (3, 0, 0, 4)), 0),
             (1, 0, 3, 0, 8, ((3, 0, 8, 5),), 0),
-            (2, 1, 6, 0, 4, ((3, 0, 4, 9),), 0),
-            (2, 1, 7, 0, 2, ((3, 0, 2, 10),), 0),
-            (6, 1, 20, 1, 1, ((8, 1, 1, 23),), 0),
-            (6, 1, 21, 1, 6, ((4, 1, 6, 22),), 0),
-            (6, 1, 22, 1, 7, ((4, 1, 7, 23),), 0),
-            (2, 1, 8, 2, 0, ((1, 1, 3, 19),), 0),
-            (2, 1, 9, 0, 10, ((3, 0, 10, 11),), 0),
+            (2, 0, 6, 0, 4, ((3, 0, 4, 9),), 0),
+            (2, 0, 7, 0, 2, ((3, 0, 2, 10),), 0),
+            (6, 0, 20, 1, 1, ((8, 1, 1, 23),), 0),
+            (6, 0, 21, 1, 6, ((4, 1, 6, 22),), 0),
+            (6, 0, 22, 1, 7, ((4, 1, 7, 23),), 0),
+            (2, 0, 8, 2, 0, ((1, 1, 3, 19),), 0),
+            (2, 0, 9, 0, 10, ((3, 0, 10, 11),), 0),
         ),
         ((0, 0, 13), (4, 0, 1), (5, 0, 9), (10, 0, 5), (11, 0, 3), (12, 0, 11), (15, 0, 15), (16, 0, 7), (17, 1, 2), (18, 1, 3), (23, 1, 4), (24, 1, 5)),
     ),
@@ -266,15 +266,15 @@
             (5, 0, 20, 1, 11, ((2, 2, 1, 22), (8, 1, 11, 25)), 0),
             (1, 0, 2, 0, 9, ((0, 0, 9, 9), (3, 0, 9, 5)), 0),
             (6, 0, 22, 1, 9, ((4, 1, 9, 24),), 0),
-            (2, 1, 6, 0, 5, ((3, 0, 5, 10),), 0),
-            (2, 1, 7, 0, 3, ((3, 0, 3, 11),), 0),
-            (6, 1, 23, 1, 8, ((8, 1, 8, 26),), 0),
-            (3, 1, 12, 1, 15, ((5, 2, 0, 18), (8, 1, 15, 17)), 0),
-            (2, 1, 8, 0, 11, ((0, 0, 11, 15), (3, 0, 11, 12)), 0),
-            (3, 1, 13, 0, 15, ((3, 0, 15, 15),), 0),
-            (3, 1, 14, 0, 7, ((3, 0, 7, 16),), 0),
-            (4, 1, 17, 2, 1, ((8, 2, 2, 21), (2, 1, 8, 19)), 0),
-            (3, 1, 15, 2, 0, ((5, 1, 11, 19),), 0),
+            (2, 0, 6, 0, 5, ((3, 0, 5, 10),), 0),
+            (2, 0, 7, 0, 3, ((3, 0, 3, 11),), 0),
+            (6, 0, 23, 1, 8, ((8, 1, 8, 26),), 0),
+            (3, 0, 12, 1, 15, ((5, 2, 0, 18), (8, 1, 15, 17)), 0),
+            (2, 0, 8, 0, 11, ((0, 0, 11, 15), (3, 0, 11, 12)), 0),
+            (3, 0, 13, 0, 15, ((3, 0, 15, 15),), 0),
+            (3, 0, 14, 0, 7, ((3, 0, 7, 16),), 0),
+            (4, 0, 17, 2, 1, ((8, 2, 2, 21), (2, 1, 8, 19)), 0),
+            (3, 0, 15, 2, 0, ((5, 1, 11, 19),), 0),
         ),
         ((0, 0, 12), (3, 0, 14), (4, 0, 0), (5, 0, 8), (9, 0, 4), (10, 0, 2), (11, 0, 10), (16, 0, 6), (18, 1, 10), (21, 1, 14), (24, 1, 12), (25, 1, 13)),
     ),
@@ -284,14 +284,14 @@
             (1, 0, 1, 0, 2, ((1, 0, 2, 7), (5, 0, 2, 7), (3, 0, 2, 4)), 0),
             (5, 0, 18, 2, 0, ((5, 1, 1, 20),), 0),
             (1, 0, 2, 0, 12, ((0, 0, 12, 8), (1, 0, 12, 8), (3, 0, 12, 5)), 0),
-            (5, 1, 19, 1, 4, ((8, 1, 4, 21),), 0),
-            (1, 1, 3, 0, 10, ((0, 0, 10, 11), (3, 0, 10, 6)), 0),
-            (5, 1, 20, 1, 5, ((8, 1, 5, 22),), 0),
-            (2, 1, 7, 0, 0, ((4, 2, 1, 17), (3, 0, 0, 10)), 0),
-            (3, 1, 13, 0, 4, ((3, 0, 4, 15),), 0),
-            (3, 1, 14, 1, 1, ((8, 1, 1, 18),), 0),
-            (2, 1, 9, 0, 8, ((3, 0, 8, 11),), 0),
-            (2, 1, 10, 0, 6, ((3, 0, 6, 12),), 0),
+            (5, 0, 19, 1, 4, ((8, 1, 4, 21),), 0),
+            (1, 0, 3, 0, 10, ((0, 0, 10, 11), (3, 0, 10, 6)), 0),
+            (5, 0, 20, 1, 5, ((8, 1, 5, 22),), 0),
+            (2, 0, 7, 0, 0, ((4, 2, 1, 17), (3, 0, 0, 10)), 0),
+            (3, 0, 13, 0, 4, ((3, 0, 4, 15),), 0),
+            (3, 0, 14, 1, 1, ((8, 1, 1, 18),), 0),
+            (2, 0, 9, 0, 8, ((3, 0, 8, 11),), 0),
+            (2, 0, 10, 0, 6, ((3, 0, 6, 12),), 0),
         ),
         ((0, 0, 15), (4, 0, 3), (5, 0, 13), (6, 0, 11), (8, 0, 1), (11, 0, 7), (12, 0, 9), (15, 1, 0), (16, 0, 5), (17, 1, 2), (21, 1, 6), (22, 1, 7), (23, 1, 3)),
     ),
@@ -309,10 +309,10 @@
             (1, 0, 3, 0, 11, ((3, 0, 11, 6),), 0),
             (6, 0, 23, 2, 3, ((2, 1, 13, 25),), 0),
             (2, 0, 7, 0, 1, ((0, 0, 1, 13), (1, 0, 1, 17), (3, 0, 1, 8)), 0),
-            (2, 1, 8, 0, 7, ((5, 0, 7, 14), (3, 0, 7, 11)), 0),
-            (6, 1, 24, 1, 15, ((4, 1, 15, 24), (8, 1, 15, 25)), 0),
-            (2, 1, 9, 0, 9, ((0, 0, 9, 17), (3, 0, 9, 12)), 0),
-            (3, 1, 13, 1, 8, ((5, 2, 1, 17), (8, 1, 8, 18)), 0),
+            (2, 0, 8, 0, 7, ((5, 0, 7, 14), (3, 0, 7, 11)), 0),
+            (6, 0, 24, 1, 15, ((4, 1, 15, 24), (8, 1, 15, 25)), 0),
+            (2, 0, 9, 0, 9, ((0, 0, 9, 17), (3, 0, 9, 12)), 0),
+            (3, 0, 13, 1, 8, ((5, 2, 1, 17), (8, 1, 8, 18)), 0),
         ),
         ((0, 0, 14), (4, 0, 2), (5, 0, 12), (6, 0, 10), (10, 0, 0), (11, 0, 8), (12, 0, 6), (15, 0, 4), (17, 1, 13), (19, 1, 11), (25, 1, 9), (26, 1, 10)),
     ),
@@ -334,7 +334,7 @@
 MB2 = 512
 NM2 = ROWS // MB2
 EARLY = NK - LAST
-START = SMAX + PER
+START = SMAX + PER - 1
 STEPS = NC + SMAX
 
 
@@ -454,11 +454,6 @@
         part = jnp.maximum(p - START, 0) % PER
         busy = jnp.logical_and(p >= START, p < START + EARLY * PER)
 
-        @pl.when(jnp.logical_and(busy, part == 0))
-        def _():
-            for i in range(PER):
-                settle(k * PER + i)
-
         @pl.loop(0, NG)
         def _(group):
             def run(g):
@@ -477,6 +472,11 @@
                         go()
 
             choose(run, 0, len(PROGRAMS))
+
+            @pl.when(jnp.logical_and(busy, part == 0))
+            def _():
+                for i in range(PER):
+                    settle(k * PER + i)
 
             if not EARLY:
                 return

time: 82.8 us -> 83.2 us (level)
  the two profiles are of different devices: /device:TPU:36 before, /device:TPU:32 now
where the time goes in v4:
time: 83.2 us; the launch traced here: 83.1 us
  Pallas kernels  82.9 us (100%)
    pallas_call x1, Pallas kernels, on_device(): pl.pallas_call(gather_kernel, out_shape=(pltpu.VMEM((NT_PTS, ROWS, COLS),...  66.3 us
    pallas_call x1, Pallas kernels, on_device(): pl.pallas_call(last_kernel, out_shape=jax.ShapeDtypeStruct((NT_PTS, ROWS,...  16.6 us

profile of v4, /device:TPU:32, one launch (start us, length us, event | category | flops | bytes accessed | tf_op | source)
XLA Modules:
  0.0 83.1 jit_solution(1317924928718613344)
XLA Ops:
  0.0 66.3 %shard_map.46 = (f32[3,2048,1024]{2,1,0:T(8,128)S(1)}, bf16[4,2048,512]{2,1,0:T(8,128)(2,1)S(1)}, bf16[4,1024,512]{2,1,0:T(8,128)(2,1)S(1)}, f32[3,2048]{1,0:T(4,128)S(1)}) custom-call(f32[3]{0:T(128)} %points.1, f32[3]{0:T(128)} %weights.1, bf16[2048,128]{1,0:T(8,128)(2,1)} %own_ref.1, f32[2048]{0:T(1024)} %den_ref.1), custom_call_target="tpu_custom_call" | custom-call | tf_op jit(solution)/shard_map/pallas_call | solution.py:542
  66.3 16.6 %shard_map.47 = f32[3,2048,1024]{2,1,0:T(8,128)} custom-call(f32[3,2048,1024]{2,1,0:T(8,128)S(1)} %get-tuple-element.9.acc, bf16[4,2048,512]{2,1,0:T(8,128)(2,1)S(1)} %get-tuple-element.10.x_ref, bf16[4,1024,512]{2,1,0:T(8,128)(2,1)S(1)} %get-tuple-element.11.y_ref, f32[3,2048]{1,0:T(4,128)S(1)} %get-tuple-element.12.f_ref), custom_call_target="tpu_custom_call" | custom-call | tf_op jit(solution)/shard_map/pallas_call | solution.py:564
